TPU v7x, 32 devices: a whole 2x2x4 slice. The times are simulated.
32 devices in a mesh: head: 2 (over core), seq: 16 (over z, y, x).
Axes of the slice: x: 2, y: 2, z: 4, core: 2. Of those that a mesh axis runs over, the one named last changes fastest.
Arguments:
- queries: bfloat16 [8192, 5120], P(('seq', 'head')), may hold values from -8 to 8
- key_states: bfloat16 [8192, 5120], P(('seq', 'head')), may hold values from -8 to 8
- value_states: bfloat16 [8192, 5120], P(('seq', 'head')), may hold values from -6 to 6
- cluster_perm: int32 [40, 8192], P('head', 'seq'), may hold values from 0 to 8191, as said below
- block_mask: int32 [40, 64, 64], P('head', 'seq'), may hold values from 0 to 1, as said below
Outputs:
- attention_out: bfloat16 [8192, 5120], P(('seq', 'head'))
Inputs may be any that keep to these rules, and one draw needn't show every extreme that they name: `cluster_perm`: for each head, positions k * 512 to (k + 1) * 512 - 1 list the tokens k * 512 to (k + 1) * 512 - 1, each once. `block_mask`: for each head and each aligned run of 4 query blocks, the key blocks used by some query block of the run number exactly 1. For such a run and the 20 heads g * 20 to (g + 1) * 20 - 1, the (head, key block) pairs so used that lie in one aligned run of 4 key blocks number at most 2, and exactly 2 in some run. Every query block uses 1 to 1 key blocks, and some query block of every run uses 1, for every head.
All inputs are finite; a program needn't handle non-finite values.
Results may differ from a plain program's by a relative error of at most 0.0049.
Values may be sent and summed in bfloat16 or wider, within the bound.
A program may use at most 128 MiB of HBM per device.

v0:
```python
import math

import jax
import jax.numpy as jnp
from jax import lax
from jax.sharding import PartitionSpec as P

HEAD_DIM = 128
BLOCK = 128


def shards(queries, key_states, value_states, cluster_perm, block_mask):
    group_heads = cluster_perm.shape[0]
    shard_rows = cluster_perm.shape[1]
    shard_blocks = shard_rows // BLOCK
    seq_count = lax.axis_size("seq")
    block_total = block_mask.shape[2]
    pick_count = max(1, block_total // 64)
    live_most = min(5, pick_count)
    capacity = max(
        1, min(shard_blocks, (group_heads * pick_count * 8 + 5 * seq_count - 1) // (5 * seq_count))
    )
    pair_count = group_heads * shard_blocks
    slot_total = seq_count * capacity
    score_scale = 1.0 / math.sqrt(HEAD_DIM)
    query_rows, key_rows, value_rows = (
        lax.all_to_all(queries, "head", split_axis=1, concat_axis=0, tiled=True),
        lax.all_to_all(key_states, "head", split_axis=1, concat_axis=0, tiled=True),
        lax.all_to_all(value_states, "head", split_axis=1, concat_axis=0, tiled=True),
    )
    local_perm = cluster_perm - lax.axis_index("seq") * shard_rows
    row_ids = jnp.arange(shard_rows, dtype=jnp.int32)
    order_table = (local_perm[:, :, None] == row_ids[None, None, :]).astype(jnp.bfloat16)
    stacked = jnp.concatenate(
        [
            query_rows.reshape(shard_rows, group_heads, HEAD_DIM),
            key_rows.reshape(shard_rows, group_heads, HEAD_DIM),
            value_rows.reshape(shard_rows, group_heads, HEAD_DIM),
        ],
        axis=2,
    )
    sorted_all = jnp.einsum(
        "hit,thd->hid", order_table, stacked, preferred_element_type=jnp.float32
    ).astype(jnp.bfloat16)
    query_sorted = sorted_all[:, :, :HEAD_DIM]
    key_sorted = sorted_all[:, :, HEAD_DIM : 2 * HEAD_DIM]
    value_sorted = sorted_all[:, :, 2 * HEAD_DIM :]
    needed = jnp.max(block_mask, axis=1)
    by_owner = needed.reshape(group_heads, seq_count, shard_blocks)
    requested = lax.all_to_all(by_owner, "seq", split_axis=1, concat_axis=1, tiled=True)

    def slot_ranks(bit_table):
        flat_bits = bit_table.transpose(1, 0, 2).reshape(seq_count, pair_count)
        return (flat_bits, jnp.cumsum(flat_bits, axis=1) - flat_bits)

    asked_bits, asked_rank = slot_ranks(requested)
    cap_ids = jnp.arange(capacity, dtype=jnp.int32)
    matches = (asked_bits[:, :, None] == 1) & (asked_rank[:, :, None] == cap_ids[None, None, :])
    send_table = matches.transpose(0, 2, 1).astype(jnp.bfloat16)
    block_width = BLOCK * HEAD_DIM
    kv_pairs = jnp.concatenate(
        [
            key_sorted.reshape(pair_count, block_width),
            value_sorted.reshape(pair_count, block_width),
        ],
        axis=1,
    )
    kv_send = jnp.einsum(
        "scp,pw->scw", send_table, kv_pairs, preferred_element_type=jnp.float32
    ).astype(jnp.bfloat16)
    key_send = kv_send[:, :, :block_width].reshape(seq_count, capacity, BLOCK, HEAD_DIM)
    value_send = kv_send[:, :, block_width:].reshape(seq_count, capacity, BLOCK, HEAD_DIM)
    own_bits, own_rank = slot_ranks(by_owner)
    prefix = jnp.cumsum(needed, axis=1) - needed
    chosen = (needed[:, :, None] == 1) & (
        prefix[:, :, None] == jnp.arange(pick_count, dtype=jnp.int32)[None, None, :]
    )
    picked = jnp.sum(
        jnp.where(chosen, jnp.arange(block_total, dtype=jnp.int32)[None, :, None], 0), axis=1
    )
    owner_idx = picked // shard_blocks
    pair_idx = (
        jnp.arange(group_heads, dtype=jnp.int32)[:, None] * shard_blocks + picked % shard_blocks
    )
    slot_idx = jnp.take(own_rank.reshape(-1), owner_idx * pair_count + pair_idx)
    position = owner_idx * capacity + slot_idx
    live_bits = jnp.take_along_axis(block_mask, picked[:, None, :], axis=2)
    query_blocks = query_sorted.reshape(group_heads, shard_blocks, BLOCK, HEAD_DIM)
    rank_live = jnp.cumsum(live_bits, axis=2) - live_bits
    selected = (live_bits[..., None] == 1) & (
        rank_live[..., None] == jnp.arange(live_most, dtype=jnp.int32)
    )
    which_pick = jnp.sum(
        jnp.where(selected, jnp.arange(pick_count, dtype=jnp.int32)[None, None, :, None], 0), axis=2
    )
    usable = jnp.any(selected, axis=2)
    key_pos = jnp.take_along_axis(
        jnp.broadcast_to(position[:, None, :], live_bits.shape), which_pick, axis=2
    )
    score_form = "qid,qljd->qilj"
    mix_form = "qilj,qljd->qid"
    slot_ids = jnp.arange(slot_total, dtype=jnp.int32)

    def select_blocks(got_flat, slot_head):
        pick_table = (slot_head[..., None] == slot_ids).astype(jnp.bfloat16)
        chosen_rows = jnp.einsum(
            "...s,sw->...w", pick_table, got_flat, preferred_element_type=jnp.float32
        ).astype(jnp.bfloat16)
        return chosen_rows.reshape(slot_head.shape + (BLOCK, HEAD_DIM))

    def head_scores(query_head, key_got, slot_head, usable_head):
        key_sel = select_blocks(key_got, slot_head)
        scores = (
            jnp.einsum(score_form, query_head, key_sel, preferred_element_type=jnp.float32)
            * score_scale
        )
        return jnp.where(usable_head[:, None, :, None], scores, -jnp.inf)

    def head_mix(weights, value_got, slot_head):
        value_sel = select_blocks(value_got, slot_head)
        return jnp.einsum(mix_form, weights, value_sel, preferred_element_type=jnp.float32).astype(
            jnp.bfloat16
        )

    flat_shape = (slot_total, block_width)
    key_got, value_got = (
        lax.all_to_all(key_send, "seq", split_axis=0, concat_axis=0, tiled=True),
        lax.all_to_all(value_send, "seq", split_axis=0, concat_axis=0, tiled=True),
    )
    key_got = key_got.reshape(flat_shape)
    value_got = value_got.reshape(flat_shape)

    def full_pass(operands):
        query_head, slot_head, usable_head = operands
        scores = head_scores(query_head, key_got, slot_head, usable_head)
        row_top = jnp.max(scores, axis=(2, 3), keepdims=True)
        exponent = jnp.exp(scores - row_top)
        row_total = jnp.sum(exponent, axis=(2, 3), keepdims=True)
        weights = (exponent / row_total).astype(jnp.bfloat16)
        return head_mix(weights, value_got, slot_head)

    attended = lax.map(full_pass, (query_blocks, key_pos, usable))
    attended_flat = attended.reshape(group_heads, shard_rows, HEAD_DIM)
    restored = jnp.einsum(
        "hit,hid->thd", order_table, attended_flat, preferred_element_type=jnp.float32
    ).astype(jnp.bfloat16)
    out_rows = restored.reshape(shard_rows, group_heads * HEAD_DIM)
    return lax.all_to_all(out_rows, "head", split_axis=0, concat_axis=1, tiled=True)


def solution(mesh):
    placed = (
        P(("seq", "head"), None),
        P(("seq", "head"), None),
        P(("seq", "head"), None),
        P("head", "seq"),
        P("head", "seq", None),
    )
    return jax.shard_map(
        shards, mesh=mesh, in_specs=placed, out_specs=P(("seq", "head"), None), check_vma=False
    )
```

profile of v0, /device:TPU:0, one launch (start us, length us, event | category | flops | bytes accessed | tf_op | source)
XLA Modules:
  0.0 286.8 jit_solution(12030051631349020649)
XLA Ops:
  0.0 4.4 %copy.43 = bf16[256,5120]{0,1:T(8,128)(2,1)} copy(bf16[256,5120]{1,0:T(8,128)(2,1)} %param.7) | data formatting | bytes 5242880 | tf_op args[0]
  4.4 4.0 %all-to-all-start = ((bf16[256,2,2560]{0,2,1:T(8,128)(2,1)}), bf16[256,2,2560]{0,2,1:T(8,128)(2,1)S(1)}, u32[]{:S(2)}, u32[]{:S(2)}) async-start(bf16[256,2,2560]{0,2,1:T(8,128)(2,1)} %bitcast.147), calls=%async_computation | async-start | bytes 5242880 | tf_op jit(solution)/shard_map/all_to_all | solution.py:27
  9.1 4.4 %copy.45 = bf16[256,5120]{0,1:T(8,128)(2,1)} copy(bf16[256,5120]{1,0:T(8,128)(2,1)} %param.8) | data formatting | bytes 5242880 | tf_op args[1]
  13.5 5.0 %all-to-all-start.1 = ((bf16[256,2,2560]{0,2,1:T(8,128)(2,1)}), bf16[256,2,2560]{0,2,1:T(8,128)(2,1)}, u32[]{:S(2)}, u32[]{:S(2)}) async-start(bf16[256,2,2560]{0,2,1:T(8,128)(2,1)} %bitcast.145), calls=%async_computation.1 | async-start | bytes 5242880 | tf_op jit(solution)/shard_map/all_to_all | solution.py:28
  18.6 17.3 %copy.44 = bf16[2,256,2560]{1,0,2:T(2,128)(2,1)} copy(bf16[2,256,2560]{1,2,0:T(8,128)(2,1)S(1)} %bitcast.143) | data formatting | bytes 5242880 | tf_op jit(solution)/shard_map/all_to_all | solution.py:27
  35.9 4.2 %reshape.468 = bf16[512,20,128]{0,2,1:T(8,128)(2,1)S(1)} reshape(bf16[2,256,2560]{1,0,2:T(2,128)(2,1)} %copy.44) | data formatting | bytes 5242880 | tf_op jit(solution)/shard_map/reshape | solution.py:36
  40.0 2.6 copy.49
  42.6 4.4 %copy.47 = bf16[256,5120]{0,1:T(8,128)(2,1)} copy(bf16[256,5120]{1,0:T(8,128)(2,1)} %param.9) | data formatting | bytes 5242880 | tf_op args[2]
  47.0 3.9 %all-to-all-start.2 = ((bf16[256,2,2560]{0,2,1:T(8,128)(2,1)}), bf16[256,2,2560]{0,2,1:T(8,128)(2,1)S(1)}, u32[]{:S(2)}, u32[]{:S(2)}) async-start(bf16[256,2,2560]{0,2,1:T(8,128)(2,1)} %bitcast.146), calls=%async_computation.2 | async-start | bytes 5242880 | tf_op jit(solution)/shard_map/all_to_all | solution.py:29
  50.8 7.0 %copy.46 = bf16[2,256,2560]{1,0,2:T(2,128)(2,1)} copy(bf16[2,256,2560]{1,2,0:T(8,128)(2,1)} %bitcast.7) | data formatting | bytes 5242880 | tf_op jit(solution)/shard_map/all_to_all | solution.py:28
  57.8 5.4 %reshape.469 = bf16[512,20,128]{0,2,1:T(8,128)(2,1)} reshape(bf16[2,256,2560]{1,0,2:T(2,128)(2,1)} %copy.46) | data formatting | bytes 5242880 | tf_op jit(solution)/shard_map/reshape | solution.py:37
  63.2 4.4 %copy.50 = bf16[512,20,128]{2,0,1:T(8,128)(2,1)} copy(bf16[512,20,128]{0,2,1:T(8,128)(2,1)} %reshape.469) | data formatting | bytes 5242880 | tf_op jit(solution)/shard_map/reshape | solution.py:37
  67.6 8.3 %all-to-all-start.3 = ((s32[20,16,4]{0,2,1:T(4,128)}), s32[20,16,4]{0,2,1:T(4,128)S(1)}, u32[]{:S(2)}, u32[]{:S(2)}) async-start(s32[20,16,4]{0,2,1:T(4,128)} %bitcast.11), calls=%async_computation.3 | async-start | bytes 65536 | tf_op jit(solution)/shard_map/all_to_all | solution.py:50
  75.9 17.3 %copy.48 = bf16[2,256,2560]{1,0,2:T(2,128)(2,1)} copy(bf16[2,256,2560]{1,2,0:T(8,128)(2,1)S(1)} %bitcast.144) | data formatting | bytes 5242880 | tf_op jit(solution)/shard_map/all_to_all | solution.py:29
  93.2 4.2 %reshape.470 = bf16[512,20,128]{0,2,1:T(8,128)(2,1)S(1)} reshape(bf16[2,256,2560]{1,0,2:T(2,128)(2,1)} %copy.48) | data formatting | bytes 5242880 | tf_op jit(solution)/shard_map/reshape | solution.py:38
  97.4 2.6 copy.51
  100.0 7.9 %fusion.39 = bf16[20,512,384]{2,1,0:T(8,128)(2,1)S(1)} fusion(bf16[512,20,128]{2,0,1:T(8,128)(2,1)} %copy.51, bf16[512,20,128]{2,0,1:T(8,128)(2,1)} %copy.50, bf16[512,20,128]{2,0,1:T(8,128)(2,1)} %copy.49, s32[20,512]{1,0:T(8,128)S(1)} %broadcast_subtract_fusion), kind=kOutput, calls=%fused_computation.46 | convolution fusion | flops 4059299840 | bytes 15769600 | tf_op jit(solution)/shard_map/hit,thd->hid/dot_general | solution.py:42
  107.8 3.1 %fusion.68 = (bf16[20,512,128]{2,1,0:T(8,128)(2,1)}, bf16[20,512,128]{2,1,0:T(8,128)(2,1)S(1)}, bf16[20,512,128]{2,1,0:T(8,128)(2,1)}) fusion(bf16[20,512,384]{2,1,0:T(8,128)(2,1)S(1)} %fusion.39), kind=kLoop, calls=%fused_computation.102 | loop fusion | bytes 15728640 | tf_op jit(solution)/shard_map/slice | solution.py:46
  110.9 5.2 %reshape.475 = bf16[80,16384]{1,0:T(8,128)(2,1)} reshape(bf16[20,512,128]{2,1,0:T(8,128)(2,1)} %get-tuple-element.99) | data formatting | bytes 5242880 | tf_op jit(solution)/shard_map/reshape | solution.py:63
  116.1 3.1 %reshape.476 = bf16[80,16384]{1,0:T(8,128)(2,1)} reshape(bf16[20,512,128]{2,1,0:T(8,128)(2,1)S(1)} %get-tuple-element.100) | data formatting | bytes 5242880 | tf_op jit(solution)/shard_map/reshape | solution.py:64
  119.7 3.4 %convolution_convert_fusion.3 = bf16[16,2,32768]{2,0,1:T(8,128)(2,1)S(1)} fusion(bf16[80,16384]{1,0:T(8,128)(2,1)} %reshape.476, bf16[80,16384]{1,0:T(8,128)(2,1)} %reshape.475, s32[16,80]{1,0:T(8,128)S(1)} %sub.46, pred[16,80]{1,0:T(8,128)(4,1)S(1)} %copy.58), kind=kOutput, calls=%fused_computation.35 | convolution fusion | flops 179311616 | bytes 7346432 | tf_op jit(solution)/shard_map/scp,pw->scw/dot_general | solution.py:68
  124.5 6.9 %all-to-all-start.4 = ((bf16[16,2,128,128]{3,2,1,0:T(8,128)(2,1)}), bf16[16,2,128,128]{3,2,1,0:T(8,128)(2,1)S(1)}, u32[]{:S(2)}, u32[]{:S(2)}) async-start(bf16[16,2,128,128]{3,2,1,0:T(8,128)(2,1)} %copy.61), calls=%async_computation.4 | async-start | bytes 2097152 | tf_op jit(solution)/shard_map/all_to_all | solution.py:127
  132.7 23.2 %all-to-all-done.4 = bf16[16,2,128,128]{3,2,1,0:T(8,128)(2,1)S(1)} async-done(((bf16[16,2,128,128]{3,2,1,0:T(8,128)(2,1)}), bf16[16,2,128,128]{3,2,1,0:T(8,128)(2,1)S(1)}, u32[]{:S(2)}, u32[]{:S(2)}) %all-to-all-start.4) | async-done | bytes 1048608 | tf_op jit(solution)/shard_map/all_to_all | solution.py:127
  155.9 5.9 %all-to-all-start.5 = ((bf16[16,2,128,128]{3,2,1,0:T(8,128)(2,1)}), bf16[16,2,128,128]{3,2,1,0:T(8,128)(2,1)S(1)}, u32[]{:S(2)}, u32[]{:S(2)}) async-start(bf16[16,2,128,128]{3,2,1,0:T(8,128)(2,1)} %copy.62), calls=%async_computation.5 | async-start | bytes 2097152 | tf_op jit(solution)/shard_map/all_to_all | solution.py:128
  166.0 1.8 gather_fusion.2
  169.5 15.3 %all-to-all-done.5 = bf16[16,2,128,128]{3,2,1,0:T(8,128)(2,1)S(1)} async-done(((bf16[16,2,128,128]{3,2,1,0:T(8,128)(2,1)}), bf16[16,2,128,128]{3,2,1,0:T(8,128)(2,1)S(1)}, u32[]{:S(2)}, u32[]{:S(2)}) %all-to-all-start.5) | async-done | bytes 1048608 | tf_op jit(solution)/shard_map/all_to_all | solution.py:128
  185.5 81.5 %while.11 = (s32[]{:T(128)}, bf16[20,4,128,128]{3,2,1,0:T(8,128)(2,1)}, pred[20,4,1]{0,1,2:T(4,128)(4,1)S(1)}, bf16[20,4,128,128]{3,2,1,0:T(8,128)(2,1)}, s32[20...) while((s32[]{:T(128)}, ...), condition=%wide.region_8.9_spmd.clone, body=%wide.region_5.8_spmd.clone.sunk | while | flops 59507712 | bytes 3936457 | solution.py:142
  186.1 1.2 fusion.99
  187.2 1.1 fusion.100
  190.1 1.2 fusion.99
  191.3 1.1 fusion.100
  194.2 1.2 fusion.99
  195.4 1.1 fusion.100
  198.3 1.2 fusion.99
  199.5 1.1 fusion.100
  202.4 1.2 fusion.99
  203.5 1.1 fusion.100
  206.4 1.2 fusion.99
  207.6 1.1 fusion.100
  210.5 1.2 fusion.99
  214.6 1.2 fusion.99
  215.8 1.1 fusion.100
  218.7 1.2 fusion.99
  222.7 1.2 fusion.99
  223.9 1.1 fusion.100
  226.8 1.2 fusion.99
  230.9 1.2 fusion.99
  232.1 1.1 fusion.100
  235.0 1.2 fusion.99
  239.1 1.2 fusion.99
  240.2 1.1 fusion.100
  243.1 1.2 fusion.99
  247.2 1.2 fusion.99
  248.4 1.1 fusion.100
  251.3 1.2 fusion.99
  255.4 1.2 fusion.99
  256.5 1.1 fusion.100
  259.4 1.2 fusion.99
  263.5 1.2 fusion.99
  264.7 1.1 fusion.100
  267.1 7.2 %convert_bitcast_fusion = bf16[512,20,128]{0,2,1:T(8,128)(2,1)} fusion(bf16[20,512,128]{2,1,0:T(8,128)(2,1)} %bitcast.162, s32[20,512]{1,0:T(8,128)S(1)} %broadcast_subtract_fusion), kind=kOutput, calls=%fused_computation.50 | convolution fusion | flops 1348730880 | bytes 5283840 | tf_op jit(solution)/shard_map/hit,hid->thd/dot_general | solution.py:144
  274.3 3.5 %all_to_all.71 = bf16[2,256,2560]{1,0,2:T(2,128)(2,1)S(1)} reshape(bf16[512,20,128]{0,2,1:T(8,128)(2,1)} %convert_bitcast_fusion) | data formatting | bytes 5242880 | tf_op jit(solution)/shard_map/all_to_all | solution.py:148
  278.2 5.8 %all_to_all.82 = bf16[2,256,2560]{1,2,0:T(8,128)(2,1)S(1)} all-to-all(bf16[2,256,2560]{1,2,0:T(8,128)(2,1)S(1)} %copy.66), channel_id=1, replica_groups=mesh['head'=2,'seq'=16] {'head'}, dimensions={0} | all-to-all | bytes 5242880 | tf_op jit(solution)/shard_map/all_to_all | solution.py:148
  284.0 2.8 copy.67
  (183 shorter events, 54.0 us)
Async XLA Ops:
  4.4 4.0 %copy-start = (s32[20,4,64]{2,1,0:T(4,128)S(1)}, s32[20,4,64]{2,1,0:T(4,128)}, u32[]{:S(2)}) copy-start(s32[20,4,64]{2,1,0:T(4,128)} %param.11) | copy-start | bytes 61444
  4.4 9.1 %all-to-all-start = ((bf16[256,2,2560]{0,2,1:T(8,128)(2,1)}), bf16[256,2,2560]{0,2,1:T(8,128)(2,1)S(1)}, u32[]{:S(2)}, u32[]{:S(2)}) async-start(bf16[256,2,2560]{0,2,1:T(8,128)(2,1)} %bitcast.147), calls=%async_computation | async-start | bytes 5242880 | tf_op jit(solution)/shard_map/all_to_all | solution.py:27
  13.5 33.5 %all-to-all-start.1 = ((bf16[256,2,2560]{0,2,1:T(8,128)(2,1)}), bf16[256,2,2560]{0,2,1:T(8,128)(2,1)}, u32[]{:S(2)}, u32[]{:S(2)}) async-start(bf16[256,2,2560]{0,2,1:T(8,128)(2,1)} %bitcast.145), calls=%async_computation.1 | async-start | bytes 5242880 | tf_op jit(solution)/shard_map/all_to_all | solution.py:28
  47.0 20.6 %all-to-all-start.2 = ((bf16[256,2,2560]{0,2,1:T(8,128)(2,1)}), bf16[256,2,2560]{0,2,1:T(8,128)(2,1)S(1)}, u32[]{:S(2)}, u32[]{:S(2)}) async-start(bf16[256,2,2560]{0,2,1:T(8,128)(2,1)} %bitcast.146), calls=%async_computation.2 | async-start | bytes 5242880 | tf_op jit(solution)/shard_map/all_to_all | solution.py:29
  67.6 51.6 %all-to-all-start.3 = ((s32[20,16,4]{0,2,1:T(4,128)}), s32[20,16,4]{0,2,1:T(4,128)S(1)}, u32[]{:S(2)}, u32[]{:S(2)}) async-start(s32[20,16,4]{0,2,1:T(4,128)} %bitcast.11), calls=%async_computation.3 | async-start | bytes 65536 | tf_op jit(solution)/shard_map/all_to_all | solution.py:50
  97.4 2.6 copy-start.1
  124.5 31.4 %all-to-all-start.4 = ((bf16[16,2,128,128]{3,2,1,0:T(8,128)(2,1)}), bf16[16,2,128,128]{3,2,1,0:T(8,128)(2,1)S(1)}, u32[]{:S(2)}, u32[]{:S(2)}) async-start(bf16[16,2,128,128]{3,2,1,0:T(8,128)(2,1)} %copy.61), calls=%async_computation.4 | async-start | bytes 2097152 | tf_op jit(solution)/shard_map/all_to_all | solution.py:127
  155.9 28.9 %all-to-all-start.5 = ((bf16[16,2,128,128]{3,2,1,0:T(8,128)(2,1)}), bf16[16,2,128,128]{3,2,1,0:T(8,128)(2,1)S(1)}, u32[]{:S(2)}, u32[]{:S(2)}) async-start(bf16[16,2,128,128]{3,2,1,0:T(8,128)(2,1)} %copy.62), calls=%async_computation.5 | async-start | bytes 2097152 | tf_op jit(solution)/shard_map/all_to_all | solution.py:128
where the time goes:
time: 290 us; the launch traced here: 287 us
  local copies, waits for them, and re-layouts  111 us (38%)
  matrix products  95.6 us (33%)
  waiting for transfers between devices  38.5 us (13%)
  starting transfers between devices  34 us (12%)
  blocking collectives  5.84 us (2%)
    sub x20, matrix products, full_pass(): exponent = jnp.exp(scores - row_top)  23.4 us
    all_to_all x1, waiting for transfers between devices, shards(): lax.all_to_all(key_send, 'seq', split_axis=0, concat_axis=0, tiled=True)  23.2 us
    dot_general x20, matrix products, head_scores(): jnp.einsum(score_form, query_head, key_sel, preferred_element_type=jnp.fl...  22.3 us
    dot_general x20, matrix products, head_mix(): jnp.einsum(mix_form, weights, value_sel, preferred_element_type=jnp.float32)  18.7 us
    all_to_all x1, local copies, waits for them, and re-layouts, shards(): lax.all_to_all(queries, 'head', split_axis=1, concat_axis=0, tiled=True)  17.3 us
    all_to_all x1, local copies, waits for them, and re-layouts, shards(): lax.all_to_all(value_states, 'head', split_axis=1, concat_axis=0, tiled=T...  17.3 us
    all_to_all x1, waiting for transfers between devices, shards(): lax.all_to_all(value_send, 'seq', split_axis=0, concat_axis=0, tiled=True)  15.3 us
    unnamed x15, local copies, waits for them, and re-layouts  15.3 us
  transfers between devices with their start and end apart: 6, of which 2 were waited for; matrix products, arithmetic and copies ran while one was open for 36% of the time, Pallas kernels for 0%

commit v1 on v0

v1 whole, which is shorter than its diff:
```python
import functools
import math

import jax
import jax.numpy as jnp
from jax import lax
from jax.experimental import pallas as pl
from jax.experimental.pallas import tpu as pltpu
from jax.sharding import PartitionSpec as P

HEAD_DIM = 128
BLOCK = 128
MESH = pl.DeviceIdType.MESH
HIGHEST = lax.Precision.HIGHEST


def iota(shape, dim):
    return lax.broadcasted_iota(jnp.int32, shape, dim)


def partner_of(me, step, count):
    if count & (count - 1):
        raise ValueError("seq size")
    peer = 0
    bit = 1
    while bit < count:
        peer = peer + bit * (((me // bit) + (step // bit)) % 2)
        bit *= 2
    return peer


def routing_kernel(shard_blocks, capacity, picks, mask_ref, req_ref, pos_ref):
    heads, _, blocks = mask_ref.shape
    seq_count = blocks // shard_blocks
    needed = jnp.max(mask_ref[...], axis=1).astype(jnp.float32)
    row, col = iota((blocks, blocks), 0), iota((blocks, blocks), 1)
    same = (row // shard_blocks) == (col // shard_blocks)
    dot = functools.partial(jnp.dot, precision=HIGHEST, preferred_element_type=jnp.float32)
    ones = lambda flag: flag.astype(jnp.float32)
    by_owner = dot(needed, ones(same))
    before_in_owner = dot(needed, ones(same & (row < col)))
    before_all = dot(needed, ones(row < col))
    lower = ones(iota((heads, heads), 1) < iota((heads, heads), 0))
    rank = dot(lower, by_owner) + before_in_owner
    head_ids, block_ids = iota((heads, blocks), 0), iota((heads, blocks), 1)
    pair = (head_ids * shard_blocks + block_ids % shard_blocks).astype(jnp.float32)
    slot_row = iota((128, blocks), 0)
    sums = jnp.zeros((128, blocks), jnp.float32)
    for c in range(capacity):
        hit = jnp.where((rank == c) & (needed > 0.5), pair, 0.0)
        sums = jnp.where(slot_row == c, jnp.sum(hit, axis=0, keepdims=True), sums)
    owner_t = ones(iota((seq_count, blocks), 1) // shard_blocks == iota((seq_count, blocks), 0))
    asked = lax.dot_general(
        owner_t, sums, (((1,), (1,)), ((), ())), precision=HIGHEST,
        preferred_element_type=jnp.float32,
    )
    req_ref[...] = (asked + 0.5).astype(jnp.int32)[:, None, :]
    position = (block_ids // shard_blocks * capacity).astype(jnp.float32) + rank
    lane = iota((heads, 128), 1)
    table = jnp.zeros((heads, 128), jnp.float32)
    for p in range(picks):
        here = jnp.where((before_all == p) & (needed > 0.5), position, 0.0)
        table = jnp.where(lane == p, jnp.sum(here, axis=1, keepdims=True), table)
    pos_ref[...] = (table + 0.5).astype(jnp.int32)


def swap_kernel(
    seq_count, pieces, key_ref, value_ref, req_ref, pos_ref,
    key_out, value_out, asked_ref, pos_out, sends, recvs, req_send, req_recv, pos_sem,
):
    group, me = lax.axis_index("head"), lax.axis_index("seq")
    other = 1 - group
    barrier = pltpu.get_barrier_semaphore()
    pl.semaphore_signal(barrier, inc=1, device_id={"head": other}, device_id_type=MESH)

    def greet(step, carry):
        pl.semaphore_signal(
            barrier, inc=1, device_id={"seq": partner_of(me, step, seq_count)}, device_id_type=MESH
        )
        return carry

    lax.fori_loop(1, seq_count, greet, 0)
    pl.semaphore_wait(barrier, seq_count)

    def ask(step):
        peer = partner_of(me, step, seq_count)
        return pltpu.make_async_remote_copy(
            src_ref=req_ref.at[peer], dst_ref=asked_ref.at[me],
            send_sem=req_send.at[step], recv_sem=req_recv.at[step],
            device_id={"seq": peer}, device_id_type=MESH,
        )

    def start(step, carry):
        ask(step).start()
        return carry

    lax.fori_loop(1, seq_count, start, 0)
    tell = pltpu.make_async_remote_copy(
        src_ref=pos_ref, dst_ref=pos_out, send_sem=pos_sem.at[0], recv_sem=pos_sem.at[1],
        device_id={"head": other}, device_id_type=MESH,
    )
    tell.start()
    rows, half = key_out.shape
    step_rows = rows // pieces
    columns = pl.ds(pl.multiple_of(other * half, 128), half)
    swaps = []
    for number, (src, dst) in enumerate(((key_ref, key_out), (value_ref, value_out))):
        for piece in range(pieces):
            part = pl.ds(piece * step_rows, step_rows)
            at = number * pieces + piece
            swaps.append(
                pltpu.make_async_remote_copy(
                    src_ref=src.at[part, columns], dst_ref=dst.at[part],
                    send_sem=sends.at[at], recv_sem=recvs.at[at],
                    device_id={"head": other}, device_id_type=MESH,
                )
            )
    for copy in swaps:
        copy.start()
    asked_ref[me] = req_ref[me]

    def finish(step, carry):
        peer = partner_of(me, step, seq_count)
        copy = pltpu.make_async_remote_copy(
            src_ref=req_ref.at[peer], dst_ref=asked_ref.at[peer],
            send_sem=req_send.at[step], recv_sem=req_recv.at[step],
            device_id={"seq": peer}, device_id_type=MESH,
        )
        copy.wait()
        return carry

    lax.fori_loop(1, seq_count, finish, 0)
    tell.wait()
    for copy in swaps:
        copy.wait()


def gather_kernel(
    shard_blocks, capacity, ids, asked, perm_ref, key_own, value_own, key_far, value_far,
    out_ref, rows_ref,
):
    group, me = ids[0], ids[1]
    step = pl.program_id(0)
    count = out_ref.shape[0]
    rows = key_own.shape[0]
    base = me * (2 * rows)
    wanted = []
    for i in range(count):
        for c in range(capacity):
            pair = asked[step * count + i, 0, c]
            head, block = pair // shard_blocks, pair % shard_blocks
            wanted.append((i, c, head))
            places = perm_ref[pl.ds(head, 1), :]
            chosen = places[:, :BLOCK]
            for b in range(1, shard_blocks):
                chosen = jnp.where(block == b, places[:, b * BLOCK : (b + 1) * BLOCK], chosen)
            rows_ref[i * capacity + c : i * capacity + c + 1, :] = chosen
    turned = rows_ref[...].T
    token = iota((BLOCK, rows), 1)
    near = token + (base + group * rows)
    far = token + (base + (1 - group) * rows)
    for i, c, head in wanted:
        at = i * capacity + c
        column = turned[:, at : at + 1]
        near_table = (column == near).astype(jnp.float32).astype(jnp.bfloat16)
        far_table = (column == far).astype(jnp.float32).astype(jnp.bfloat16)
        columns = pl.ds(pl.multiple_of(head * HEAD_DIM, HEAD_DIM), HEAD_DIM)
        for which, (own, away) in enumerate(((key_own, key_far), (value_own, value_far))):
            got = jnp.dot(near_table, own[:, columns], preferred_element_type=jnp.float32)
            got += jnp.dot(far_table, away[:, columns], preferred_element_type=jnp.float32)
            out_ref[i, c, :, which * HEAD_DIM : (which + 1) * HEAD_DIM] = got.astype(jnp.bfloat16)


def exchange_kernel(seq_count, send_ref, got_ref, sends, recvs, relay_send, relay_recv, own_sem):
    group, me = lax.axis_index("head"), lax.axis_index("seq")
    other = 1 - group
    barrier = pltpu.get_barrier_semaphore()
    pl.semaphore_signal(barrier, inc=1, device_id={"head": other}, device_id_type=MESH)

    def greet(step, carry):
        pl.semaphore_signal(
            barrier, inc=1, device_id={"seq": partner_of(me, step, seq_count)}, device_id_type=MESH
        )
        return carry

    lax.fori_loop(1, seq_count, greet, 0)
    pl.semaphore_wait(barrier, seq_count)

    def deliver(step, landing):
        peer = partner_of(me, step, seq_count)
        return pltpu.make_async_remote_copy(
            src_ref=send_ref.at[peer], dst_ref=got_ref.at[0, peer if landing else me],
            send_sem=sends.at[step], recv_sem=recvs.at[step],
            device_id={"seq": peer}, device_id_type=MESH,
        )

    def relay(step):
        peer = partner_of(me, step, seq_count)
        return pltpu.make_async_remote_copy(
            src_ref=got_ref.at[0, peer], dst_ref=got_ref.at[1, peer],
            send_sem=relay_send.at[step], recv_sem=relay_recv.at[step],
            device_id={"head": other}, device_id_type=MESH,
        )

    def start(i, carry):
        deliver(seq_count - 1 - i, False).start()
        return carry

    lax.fori_loop(0, seq_count - 1, start, 0)
    mine = pltpu.make_async_copy(send_ref.at[me], got_ref.at[0, me], own_sem)
    mine.start()
    share = pltpu.make_async_remote_copy(
        src_ref=send_ref.at[me], dst_ref=got_ref.at[1, me],
        send_sem=relay_send.at[0], recv_sem=relay_recv.at[0],
        device_id={"head": other}, device_id_type=MESH,
    )
    share.start()

    def pass_on(i, carry):
        step = seq_count - 1 - i
        deliver(step, True).wait_recv()
        relay(step).start()
        return carry

    lax.fori_loop(0, seq_count - 1, pass_on, 0)

    def finish(step, carry):
        deliver(step, True).wait_send()
        relay(step).wait()
        return carry

    lax.fori_loop(1, seq_count, finish, 0)
    mine.wait()
    share.wait()


def attend_kernel(heads, picks, slots, masked, ids, pos_own, pos_far, *refs):
    if masked:
        query_ref, kv_ref, allow_ref, out_ref = refs
    else:
        query_ref, kv_ref, out_ref = refs
    group = ids[0]
    width = query_ref.shape[1] // HEAD_DIM
    scale = 1.0 / math.sqrt(HEAD_DIM)
    for w in range(width):
        head = pl.program_id(0) * width + w
        away = (head // heads) != group
        local = head % heads
        columns = slice(w * HEAD_DIM, (w + 1) * HEAD_DIM)
        query = query_ref[:, columns]
        scores, values = [], []
        for p in range(picks):
            slot = jnp.where(away, pos_far[local, p] + slots, pos_own[local, p])
            key = kv_ref[slot, :, :HEAD_DIM]
            values.append(kv_ref[slot, :, HEAD_DIM:])
            score = lax.dot_general(
                query, key, (((1,), (1,)), ((), ())), preferred_element_type=jnp.float32
            ) * scale
            if masked:
                score = jnp.where(allow_ref[w, :, p : p + 1] > 0, score, -jnp.inf)
            scores.append(score)
        top = jnp.max(scores[0], axis=1, keepdims=True)
        for score in scores[1:]:
            top = jnp.maximum(top, jnp.max(score, axis=1, keepdims=True))
        exps = [jnp.exp(score - top) for score in scores]
        total = jnp.sum(exps[0], axis=1, keepdims=True)
        for e in exps[1:]:
            total = total + jnp.sum(e, axis=1, keepdims=True)
        inverse = 1.0 / total
        mixed = None
        for e, value in zip(exps, values):
            part = jnp.dot(
                (e * inverse).astype(jnp.bfloat16), value, preferred_element_type=jnp.float32
            )
            mixed = part if mixed is None else mixed + part
        out_ref[:, columns] = mixed.astype(jnp.bfloat16)


def token_allow(cluster_perm, block_mask, picks, me, shard_rows):
    needed = jnp.max(block_mask, axis=1)
    prefix = jnp.cumsum(needed, axis=1) - needed
    chosen = (needed[:, :, None] == 1) & (prefix[:, :, None] == jnp.arange(picks)[None, None, :])
    live = jnp.einsum(
        "hqb,hbp->hqp", block_mask.astype(jnp.float32), chosen.astype(jnp.float32)
    )
    group_heads = cluster_perm.shape[0]
    local = cluster_perm - me * shard_rows
    place = jnp.zeros((group_heads, shard_rows), jnp.int32)
    place = place.at[jnp.arange(group_heads)[:, None], local].set(
        jnp.broadcast_to(jnp.arange(shard_rows, dtype=jnp.int32) // BLOCK, local.shape)
    )
    by_token = jnp.take_along_axis(live, place[:, :, None], axis=1).astype(jnp.float32)
    return lax.all_to_all(by_token, "head", split_axis=1, concat_axis=0, tiled=True)


def shards(queries, key_states, value_states, cluster_perm, block_mask):
    group_heads, shard_rows = cluster_perm.shape
    shard_blocks = shard_rows // BLOCK
    seq_count = lax.axis_size("seq")
    block_total = block_mask.shape[2]
    picks = max(1, block_total // 64)
    capacity = max(
        1, min(shard_blocks, (group_heads * picks * 8 + 5 * seq_count - 1) // (5 * seq_count))
    )
    slots = seq_count * capacity
    rows, columns = queries.shape
    half = columns // 2
    group, me = lax.axis_index("head"), lax.axis_index("seq")
    ids = jnp.stack([group, me]).astype(jnp.int32)
    vmem = pl.BlockSpec(memory_space=pltpu.VMEM)
    smem = pl.BlockSpec(memory_space=pltpu.SMEM)
    anywhere = pl.BlockSpec(memory_space=pl.ANY)
    struct = jax.ShapeDtypeStruct
    bf16, i32 = jnp.bfloat16, jnp.int32

    requests, positions = pl.pallas_call(
        functools.partial(routing_kernel, shard_blocks, capacity, picks),
        out_shape=(struct((seq_count, 1, 128), i32), struct((group_heads, 128), i32)),
        in_specs=[vmem], out_specs=(vmem, vmem), name="routing",
    )(block_mask)

    pieces = 4
    dma = pltpu.SemaphoreType.DMA
    key_far, value_far, asked, pos_far = pl.pallas_call(
        functools.partial(swap_kernel, seq_count, pieces),
        out_shape=(
            struct((rows, half), bf16), struct((rows, half), bf16),
            struct((seq_count, 1, 128), i32), struct((group_heads, 128), i32),
        ),
        in_specs=[anywhere, anywhere, vmem, vmem],
        out_specs=(anywhere, anywhere, vmem, vmem),
        scratch_shapes=[
            dma((2 * pieces,)), dma((2 * pieces,)), dma((seq_count,)), dma((seq_count,)), dma((2,)),
        ],
        compiler_params=pltpu.CompilerParams(collective_id=0, has_side_effects=True),
        name="swap",
    )(key_states, value_states, requests, positions)

    steps = 4 if seq_count % 4 == 0 else 1
    share = seq_count // steps
    own_half = pl.BlockSpec((rows, half), lambda i, ids, asked: (0, ids[0]))
    whole_half = pl.BlockSpec((rows, half), lambda i, ids, asked: (0, 0))
    to_send = pl.pallas_call(
        functools.partial(gather_kernel, shard_blocks, capacity),
        out_shape=struct((seq_count, capacity, BLOCK, 2 * HEAD_DIM), bf16),
        grid_spec=pltpu.PrefetchScalarGridSpec(
            num_scalar_prefetch=2,
            grid=(steps,),
            in_specs=[
                pl.BlockSpec((group_heads, shard_rows), lambda i, ids, asked: (0, 0)),
                own_half, own_half, whole_half, whole_half,
            ],
            out_specs=pl.BlockSpec(
                (share, capacity, BLOCK, 2 * HEAD_DIM), lambda i, ids, asked: (i, 0, 0, 0)
            ),
            scratch_shapes=[pltpu.VMEM((128, 128), i32)],
        ),
        name="gather",
    )(ids, asked, cluster_perm, key_states, value_states, key_far, value_far)

    got = pl.pallas_call(
        functools.partial(exchange_kernel, seq_count),
        out_shape=struct((2, seq_count, capacity, BLOCK, 2 * HEAD_DIM), bf16),
        in_specs=[anywhere], out_specs=anywhere,
        scratch_shapes=[dma((seq_count,)) for _ in range(4)] + [dma],
        compiler_params=pltpu.CompilerParams(collective_id=1, has_side_effects=True),
        name="exchange",
    )(to_send)
    got = got.reshape(2 * slots, BLOCK, 2 * HEAD_DIM)

    masked = picks > 1
    total_heads = columns // HEAD_DIM
    width = 8 if total_heads % 8 == 0 else 1
    in_specs = [
        pl.BlockSpec((rows, width * HEAD_DIM), lambda i, *_: (0, i)),
        pl.BlockSpec(got.shape, lambda i, *_: (0, 0, 0)),
    ]
    operands = [queries, got]
    if masked:
        in_specs.append(pl.BlockSpec((width, rows, picks), lambda i, *_: (i, 0, 0)))
        operands.append(token_allow(cluster_perm, block_mask, picks, me, shard_rows))
    return pl.pallas_call(
        functools.partial(attend_kernel, group_heads, picks, slots, masked),
        out_shape=struct((rows, columns), bf16),
        grid_spec=pltpu.PrefetchScalarGridSpec(
            num_scalar_prefetch=3,
            grid=(total_heads // width,),
            in_specs=in_specs,
            out_specs=pl.BlockSpec((rows, width * HEAD_DIM), lambda i, *_: (0, i)),
        ),
        compiler_params=pltpu.CompilerParams(vmem_limit_bytes=56 * 1024 * 1024),
        name="attend",
    )(ids, positions, pos_far, *operands)


def solution(mesh):
    rows = P(("seq", "head"), None)
    placed = (rows, rows, rows, P("head", "seq"), P("head", "seq", None))
    return jax.shard_map(shards, mesh=mesh, in_specs=placed, out_specs=rows, check_vma=False)
```

time: 290 us -> 90.2 us (0.31)
  local copies, waits for them, and re-layouts: 111 us -> 0 us
  matrix products: 95.6 us -> 0 us
  Pallas kernels: 0 us -> 89.2 us
  waiting for transfers between devices: 38.5 us -> 0 us
  starting transfers between devices: 34 us -> 0 us
  blocking collectives: 5.84 us -> 0 us
    pallas_call x0 -> x5, Pallas kernels: none -> 89.2 us  [the longest x1 55.5 us: shards(): pl.pallas_call(functools.partial(exchange_kernel, seq_count), out_shape=s...]
    dot_general x83 -> x0, matrix products: 72.2 us -> none  [the longest x20 22.3 us: head_scores(): jnp.einsum(score_form, query_head, key_sel, preferred_element_type=jnp.fl...]
    all_to_all x6 -> x0, local copies, waits for them, and re-layouts: 48.2 us -> none  [the longest x1 17.3 us: shards(): lax.all_to_all(queries, 'head', split_axis=1, concat_axis=0, tiled=True)]
    all_to_all x6 -> x0, waiting for transfers between devices: 38.5 us -> none  [the longest x1 23.2 us: shards(): lax.all_to_all(key_send, 'seq', split_axis=0, concat_axis=0, tiled=True)]
    all_to_all x6 -> x0, starting transfers between devices: 34 us -> none  [the longest x1 8.35 us: shards(): lax.all_to_all(by_owner, 'seq', split_axis=1, concat_axis=1, tiled=True)]
    reshape x12 -> x0, local copies, waits for them, and re-layouts: 33.8 us -> none  [the longest x2 9.76 us: shards(): key_rows.reshape(shard_rows, group_heads, HEAD_DIM)]
    sub x20 -> x0, matrix products: 23.4 us -> none  [full_pass(): exponent = jnp.exp(scores - row_top)]
    unnamed x15 -> x0, local copies, waits for them, and re-layouts: 15.3 us -> none
  transfers between devices with their start and end apart: 6 -> 0, of which waited for: 2 -> 0; matrix products, arithmetic and copies ran while one was open for 36% -> 0% of each run, Pallas kernels for 0% -> 0%
where the time goes in v1:
time: 90.2 us; the launch traced here: 89.8 us
  Pallas kernels  89.2 us (99%)
    pallas_call x1, Pallas kernels, shards(): pl.pallas_call(functools.partial(exchange_kernel, seq_count), out_shape=s...  55.5 us
    pallas_call x1, Pallas kernels, shards(): pl.pallas_call(functools.partial(swap_kernel, seq_count, pieces), out_sha...  13.6 us
    pallas_call x1, Pallas kernels, shards(): pl.pallas_call(functools.partial(attend_kernel, group_heads, picks, slots...  10.2 us
    pallas_call x1, Pallas kernels, shards(): pl.pallas_call(functools.partial(gather_kernel, shard_blocks, capacity),...  7.86 us
    pallas_call x1, Pallas kernels, shards(): pl.pallas_call(functools.partial(routing_kernel, shard_blocks, capacity,...  1.91 us

profile of v1, /device:TPU:0, one launch (start us, length us, event | category | flops | bytes accessed | tf_op | source)
XLA Modules:
  0.0 89.8 jit_solution(15379841628061266968)
XLA Ops:
  0.0 0.6 pad_add_fusion.ids
  0.6 1.9 %routing.1 = (s32[16,1,128]{2,1,0:T(1,128)}, s32[20,128]{1,0:T(8,128)}) custom-call(s32[20,4,64]{2,1,0:T(4,128)} %mask_ref.1), custom_call_target="tpu_custom_call" | custom-call | tf_op jit(solution)/shard_map/routing/pallas_call | solution.py:316
  2.5 13.6 %swap.1 = (bf16[256,2560]{1,0:T(8,128)(2,1)}, bf16[256,2560]{1,0:T(8,128)(2,1)}, s32[16,1,128]{2,1,0:T(1,128)}, s32[20,128]{1,0:T(8,128)}) custom-call(bf16[256,5120]{1,0:T(8,128)(2,1)} %key_own.1, bf16[256,5120]{1,0:T(8,128)(2,1)} %value_own.1, s32[16,1,128]{2,1,0:T(1,128)} %get-tuple-element.12.req_ref, s32[20,128]{1,0:T(8,128)} %get-tuple-element.11.pos_ref.pos_own), custom_call_target="tpu_custom_call" | custom-call | tf_op jit(solution)/shard_map/swap/pallas_call | solution.py:324
  16.1 7.9 %gather.1.send_ref = bf16[16,2,128,256]{3,2,1,0:T(8,128)(2,1)} custom-call(s32[2]{0:T(128)} %pad_add_fusion.ids, s32[16,1,128]{2,1,0:T(1,128)} %get-tuple-element.14.asked, s32[20,512]{1,0:T(8,128)} %perm_ref.1, bf16[256,5120]{1,0:T(8,128)(2,1)} %key_own.1, bf16[256,5120]{1,0:T(8,128)(2,1)} %value_own.1, bf16[256,2560]{1,0:T(8,128)(2,1)} %get-tuple-element.15.key_far, ...), custom_call_target="tpu_custom_call" | custom-call | tf_op jit(solution)/shard_map/gather/pallas_call | solution.py:343
  24.0 55.5 %exchange.1 = bf16[2,16,2,128,256]{4,3,2,1,0:T(8,128)(2,1)} custom-call(bf16[16,2,128,256]{3,2,1,0:T(8,128)(2,1)} %gather.1.send_ref), custom_call_target="tpu_custom_call" | custom-call | tf_op jit(solution)/shard_map/exchange/pallas_call | solution.py:361
  79.5 10.2 %attend.1 = bf16[256,5120]{1,0:T(8,128)(2,1)} custom-call(s32[2]{0:T(128)} %pad_add_fusion.ids, s32[20,128]{1,0:T(8,128)} %get-tuple-element.11.pos_ref.pos_own, s32[20,128]{1,0:T(8,128)} %get-tuple-element.13.pos_far, bf16[256,5120]{1,0:T(8,128)(2,1)} %refs_0_.1, bf16[64,128,256]{2,1,0:T(8,128)(2,1)} %bitcast.3), custom_call_target="tpu_custom_call" | custom-call | tf_op jit(solution)/shard_map/attend/pallas_call | solution.py:382

commit v2 on v1

v2 whole, which is shorter than its diff:
```python
import functools
import math

import jax
import jax.numpy as jnp
from jax import lax
from jax.experimental import pallas as pl
from jax.experimental.pallas import tpu as pltpu
from jax.sharding import PartitionSpec as P

HEAD_DIM = 128
BLOCK = 128
MESH = pl.DeviceIdType.MESH
HIGHEST = lax.Precision.HIGHEST


def iota(shape, dim):
    return lax.broadcasted_iota(jnp.int32, shape, dim)


def partner_of(me, step, count):
    if count & (count - 1):
        raise ValueError("seq size")
    peer = 0
    bit = 1
    while bit < count:
        peer = peer + bit * (((me // bit) + (step // bit)) % 2)
        bit *= 2
    return peer


def routing_kernel(shard_blocks, capacity, picks, mask_ref, req_ref, pos_ref):
    heads, _, blocks = mask_ref.shape
    seq_count = blocks // shard_blocks
    needed = jnp.max(mask_ref[...], axis=1).astype(jnp.float32)
    row, col = iota((blocks, blocks), 0), iota((blocks, blocks), 1)
    same = (row // shard_blocks) == (col // shard_blocks)
    dot = functools.partial(jnp.dot, precision=HIGHEST, preferred_element_type=jnp.float32)
    ones = lambda flag: flag.astype(jnp.float32)
    by_owner = dot(needed, ones(same))
    before_in_owner = dot(needed, ones(same & (row < col)))
    before_all = dot(needed, ones(row < col))
    lower = ones(iota((heads, heads), 1) < iota((heads, heads), 0))
    rank = dot(lower, by_owner) + before_in_owner
    head_ids, block_ids = iota((heads, blocks), 0), iota((heads, blocks), 1)
    pair = (head_ids * shard_blocks + block_ids % shard_blocks).astype(jnp.float32)
    slot_row = iota((128, blocks), 0)
    sums = jnp.zeros((128, blocks), jnp.float32)
    for c in range(capacity):
        hit = jnp.where((rank == c) & (needed > 0.5), pair, 0.0)
        sums = jnp.where(slot_row == 2 * c, jnp.sum(hit, axis=0, keepdims=True), sums)
        hit = jnp.where((rank == c) & (needed > 0.5), head_ids.astype(jnp.float32), 0.0)
        sums = jnp.where(slot_row == 2 * c + 1, jnp.sum(hit, axis=0, keepdims=True), sums)
    owner_t = ones(iota((seq_count, blocks), 1) // shard_blocks == iota((seq_count, blocks), 0))
    asked = lax.dot_general(
        owner_t, sums, (((1,), (1,)), ((), ())), precision=HIGHEST,
        preferred_element_type=jnp.float32,
    )
    req_ref[...] = (asked + 0.5).astype(jnp.int32)[:, None, :]
    position = (block_ids // shard_blocks * capacity).astype(jnp.float32) + rank
    lane = iota((heads, 128), 1)
    table = jnp.zeros((heads, 128), jnp.float32)
    for p in range(picks):
        here = jnp.where((before_all == p) & (needed > 0.5), position, 0.0)
        table = jnp.where(lane == p, jnp.sum(here, axis=1, keepdims=True), table)
    pos_ref[...] = (table + 0.5).astype(jnp.int32)


def order(i, me, count):
    top, next_bit = (me // (count // 2)) % 2, (me // (count // 4)) % 2
    end = (top + next_bit + 1) % 2
    return end * (1 + (i + count // 4 - 1) % (count - 1)) + (1 - end) * (count - 1 - i)


def exchange_kernel(
    seq_count, capacity,
    key_ref, value_ref, perm_ref, req_ref, pos_ref, got_ref, pos_out,
    near_kv, far_kv, asked_ref, asked, send_ref, rows_ref,
    load_sem, swap_send, swap_recv, req_send, req_recv, misc_sem,
    sends, recvs, relay_send, relay_recv,
):
    group, me = lax.axis_index("head"), lax.axis_index("seq")
    other = 1 - group
    heads, rows = near_kv.shape[1:3]
    barrier = pltpu.get_barrier_semaphore()
    pl.semaphore_signal(barrier, inc=1, device_id={"head": other}, device_id_type=MESH)

    def greet(step, carry):
        pl.semaphore_signal(
            barrier, inc=1, device_id={"seq": partner_of(me, step, seq_count)}, device_id_type=MESH
        )
        return carry

    lax.fori_loop(1, seq_count, greet, 0)
    loads = []
    for number, src in enumerate((key_ref, value_ref)):
        for head in range(heads):
            start_at = pl.multiple_of((group * heads + head) * HEAD_DIM, HEAD_DIM)
            loads.append(
                pltpu.make_async_copy(
                    src.at[:, pl.ds(start_at, HEAD_DIM)], near_kv.at[number, head],
                    load_sem.at[number * heads + head],
                )
            )
    for copy in loads:
        copy.start()
    pl.semaphore_wait(barrier, seq_count)

    def ask(step, landing):
        peer = partner_of(me, step, seq_count)
        return pltpu.make_async_remote_copy(
            src_ref=req_ref.at[peer], dst_ref=asked_ref.at[peer if landing else me],
            send_sem=req_send.at[step], recv_sem=req_recv.at[step],
            device_id={"seq": peer}, device_id_type=MESH,
        )

    def start_ask(step, carry):
        ask(step, False).start()
        return carry

    lax.fori_loop(1, seq_count, start_ask, 0)
    swaps = []
    for number, src in enumerate((key_ref, value_ref)):
        for head in range(heads):
            start_at = pl.multiple_of((other * heads + head) * HEAD_DIM, HEAD_DIM)
            at = number * heads + head
            swaps.append(
                pltpu.make_async_remote_copy(
                    src_ref=src.at[:, pl.ds(start_at, HEAD_DIM)], dst_ref=far_kv.at[number, head],
                    send_sem=swap_send.at[at], recv_sem=swap_recv.at[at],
                    device_id={"head": other}, device_id_type=MESH,
                )
            )
    for copy in swaps:
        copy.start()
    tell = pltpu.make_async_remote_copy(
        src_ref=pos_ref, dst_ref=pos_out, send_sem=misc_sem.at[0], recv_sem=misc_sem.at[1],
        device_id={"head": other}, device_id_type=MESH,
    )
    tell.start()
    keep = pltpu.make_async_copy(req_ref.at[me], asked_ref.at[me], misc_sem.at[2])
    keep.start()
    keep.wait()

    def finish_ask(step, carry):
        ask(step, True).wait()
        return carry

    lax.fori_loop(1, seq_count, finish_ask, 0)
    to_scalar = pltpu.make_async_copy(asked_ref, asked, misc_sem.at[3])
    to_scalar.start()
    to_scalar.wait()
    for copy in loads:
        copy.wait()
    for copy in swaps:
        copy.wait()

    base = me * (2 * rows)
    token = iota((BLOCK, rows), 1)
    near = token + (base + group * rows)
    far = token + (base + other * rows)
    rows_ref[...] = jnp.zeros_like(rows_ref)

    def gather(peer):
        chosen = []
        for c in range(capacity):
            rows_ref[c : c + 1, :] = perm_ref[asked[peer, 0, 2 * c]]
            chosen.append(asked[peer, 0, 2 * c + 1])
        turned = rows_ref[...].T
        for c, head in enumerate(chosen):
            column = turned[:, c : c + 1]
            near_table = (column == near).astype(jnp.float32).astype(jnp.bfloat16)
            far_table = (column == far).astype(jnp.float32).astype(jnp.bfloat16)
            for which in range(2):
                got = jnp.dot(near_table, near_kv[which, head], preferred_element_type=jnp.float32)
                got += jnp.dot(far_table, far_kv[which, head], preferred_element_type=jnp.float32)
                send_ref[peer, c, :, which * HEAD_DIM : (which + 1) * HEAD_DIM] = got.astype(
                    jnp.bfloat16
                )

    def deliver(step, landing):
        peer = partner_of(me, step, seq_count)
        return pltpu.make_async_remote_copy(
            src_ref=send_ref.at[peer], dst_ref=got_ref.at[0, peer if landing else me],
            send_sem=sends.at[step], recv_sem=recvs.at[step],
            device_id={"seq": peer}, device_id_type=MESH,
        )

    def relay(step):
        peer = partner_of(me, step, seq_count)
        return pltpu.make_async_remote_copy(
            src_ref=got_ref.at[0, peer], dst_ref=got_ref.at[1, peer],
            send_sem=relay_send.at[step], recv_sem=relay_recv.at[step],
            device_id={"head": other}, device_id_type=MESH,
        )

    gather(partner_of(me, order(0, me, seq_count), seq_count))

    def produce(i, carry):
        gather(partner_of(me, order(i, me, seq_count), seq_count))
        deliver(order(i - 1, me, seq_count), False).start()
        return carry

    lax.fori_loop(1, seq_count - 1, produce, 0)
    gather(me)
    deliver(order(seq_count - 2, me, seq_count), False).start()

    def pass_on(i, carry):
        step = order(i, me, seq_count)
        deliver(step, True).wait_recv()
        relay(step).start()
        return carry

    pass_on(0, 0)
    mine = pltpu.make_async_copy(send_ref.at[me], got_ref.at[0, me], misc_sem.at[4])
    mine.start()
    share = pltpu.make_async_remote_copy(
        src_ref=send_ref.at[me], dst_ref=got_ref.at[1, me],
        send_sem=relay_send.at[0], recv_sem=relay_recv.at[0],
        device_id={"head": other}, device_id_type=MESH,
    )
    share.start()
    lax.fori_loop(1, seq_count - 1, pass_on, 0)

    def finish(step, carry):
        deliver(step, True).wait_send()
        relay(step).wait()
        return carry

    lax.fori_loop(1, seq_count, finish, 0)
    mine.wait()
    share.wait()
    tell.wait()


def attend_kernel(heads, picks, slots, masked, ids, pos_own, pos_far, *refs):
    if masked:
        query_ref, kv_ref, allow_ref, out_ref = refs
    else:
        query_ref, kv_ref, out_ref = refs
    group = ids[0]
    width = query_ref.shape[1] // HEAD_DIM
    scale = 1.0 / math.sqrt(HEAD_DIM)
    slot_of, scores = [], []
    for w in range(width):
        head = pl.program_id(0) * width + w
        away = (head // heads) != group
        local = head % heads
        query = query_ref[:, w * HEAD_DIM : (w + 1) * HEAD_DIM]
        for p in range(picks):
            slot = jnp.where(away, pos_far[local, p] + slots, pos_own[local, p])
            slot_of.append(slot)
            score = lax.dot_general(
                query, kv_ref[slot, :, :HEAD_DIM], (((1,), (1,)), ((), ())),
                preferred_element_type=jnp.float32,
            ) * scale
            if masked:
                score = jnp.where(allow_ref[w, :, p : p + 1] > 0, score, -jnp.inf)
            scores.append(score)
    weights = []
    for w in range(width):
        own = scores[w * picks : (w + 1) * picks]
        top = functools.reduce(jnp.maximum, [jnp.max(s, axis=1, keepdims=True) for s in own])
        exps = [jnp.exp(s - top) for s in own]
        total = functools.reduce(jnp.add, [jnp.sum(e, axis=1, keepdims=True) for e in exps])
        inverse = 1.0 / total
        weights.extend([(e * inverse).astype(jnp.bfloat16) for e in exps])
    mixed = []
    for w in range(width):
        parts = [
            jnp.dot(
                weights[w * picks + p], kv_ref[slot_of[w * picks + p], :, HEAD_DIM:],
                preferred_element_type=jnp.float32,
            )
            for p in range(picks)
        ]
        mixed.append(functools.reduce(jnp.add, parts).astype(jnp.bfloat16))
    for w in range(width):
        out_ref[:, w * HEAD_DIM : (w + 1) * HEAD_DIM] = mixed[w]


def token_allow(cluster_perm, block_mask, picks, me, shard_rows):
    needed = jnp.max(block_mask, axis=1)
    prefix = jnp.cumsum(needed, axis=1) - needed
    chosen = (needed[:, :, None] == 1) & (prefix[:, :, None] == jnp.arange(picks)[None, None, :])
    live = jnp.einsum(
        "hqb,hbp->hqp", block_mask.astype(jnp.float32), chosen.astype(jnp.float32)
    )
    group_heads = cluster_perm.shape[0]
    local = cluster_perm - me * shard_rows
    place = jnp.zeros((group_heads, shard_rows), jnp.int32)
    place = place.at[jnp.arange(group_heads)[:, None], local].set(
        jnp.broadcast_to(jnp.arange(shard_rows, dtype=jnp.int32) // BLOCK, local.shape)
    )
    by_token = jnp.take_along_axis(live, place[:, :, None], axis=1).astype(jnp.float32)
    return lax.all_to_all(by_token, "head", split_axis=1, concat_axis=0, tiled=True)


def shards(queries, key_states, value_states, cluster_perm, block_mask):
    group_heads, shard_rows = cluster_perm.shape
    shard_blocks = shard_rows // BLOCK
    seq_count = lax.axis_size("seq")
    block_total = block_mask.shape[2]
    picks = max(1, block_total // 64)
    capacity = max(
        1, min(shard_blocks, (group_heads * picks * 8 + 5 * seq_count - 1) // (5 * seq_count))
    )
    slots = seq_count * capacity
    rows, columns = queries.shape
    group, me = lax.axis_index("head"), lax.axis_index("seq")
    ids = jnp.stack([group, me]).astype(jnp.int32)
    vmem = pl.BlockSpec(memory_space=pltpu.VMEM)
    smem = pl.BlockSpec(memory_space=pltpu.SMEM)
    anywhere = pl.BlockSpec(memory_space=pl.ANY)
    struct = jax.ShapeDtypeStruct
    bf16, i32 = jnp.bfloat16, jnp.int32

    requests, positions = pl.pallas_call(
        functools.partial(routing_kernel, shard_blocks, capacity, picks),
        out_shape=(struct((seq_count, 1, 128), i32), struct((group_heads, 128), i32)),
        in_specs=[vmem], out_specs=(vmem, vmem), name="routing",
    )(block_mask)

    dma = pltpu.SemaphoreType.DMA
    perm_blocks = cluster_perm.reshape(group_heads * shard_blocks, 1, BLOCK)
    kv_half = pltpu.VMEM((2, group_heads, rows, HEAD_DIM), bf16)
    got, pos_far = pl.pallas_call(
        functools.partial(exchange_kernel, seq_count, capacity),
        out_shape=(
            struct((2, seq_count, capacity, BLOCK, 2 * HEAD_DIM), bf16),
            struct((group_heads, 128), i32),
        ),
        in_specs=[anywhere, anywhere, vmem, vmem, vmem],
        out_specs=(anywhere, vmem),
        scratch_shapes=[
            kv_half, kv_half,
            pltpu.VMEM((seq_count, 1, 128), i32),
            pltpu.SMEM((seq_count, 1, 128), i32),
            pltpu.VMEM((seq_count, capacity, BLOCK, 2 * HEAD_DIM), bf16),
            pltpu.VMEM((8 * -(-capacity // 8), 128), i32),
            dma((2 * group_heads,)), dma((2 * group_heads,)), dma((2 * group_heads,)),
            dma((seq_count,)), dma((seq_count,)), dma((5,)),
        ] + [dma((seq_count,)) for _ in range(4)],
        compiler_params=pltpu.CompilerParams(collective_id=0, has_side_effects=True),
        name="exchange",
    )(key_states, value_states, perm_blocks, requests, positions)
    got = got.reshape(2 * slots, BLOCK, 2 * HEAD_DIM)

    masked = picks > 1
    total_heads = columns // HEAD_DIM
    width = 8 if total_heads % 8 == 0 else 1
    in_specs = [
        pl.BlockSpec((rows, width * HEAD_DIM), lambda i, *_: (0, i)),
        pl.BlockSpec(got.shape, lambda i, *_: (0, 0, 0)),
    ]
    operands = [queries, got]
    if masked:
        in_specs.append(pl.BlockSpec((width, rows, picks), lambda i, *_: (i, 0, 0)))
        operands.append(token_allow(cluster_perm, block_mask, picks, me, shard_rows))
    return pl.pallas_call(
        functools.partial(attend_kernel, group_heads, picks, slots, masked),
        out_shape=struct((rows, columns), bf16),
        grid_spec=pltpu.PrefetchScalarGridSpec(
            num_scalar_prefetch=3,
            grid=(total_heads // width,),
            in_specs=in_specs,
            out_specs=pl.BlockSpec((rows, width * HEAD_DIM), lambda i, *_: (0, i)),
        ),
        compiler_params=pltpu.CompilerParams(vmem_limit_bytes=56 * 1024 * 1024),
        name="attend",
    )(ids, positions, pos_far, *operands)


def solution(mesh):
    rows = P(("seq", "head"), None)
    placed = (rows, rows, rows, P("head", "seq"), P("head", "seq", None))
    return jax.shard_map(shards, mesh=mesh, in_specs=placed, out_specs=rows, check_vma=False)
```

time: 90.2 us -> 81.3 us (0.901)
  Pallas kernels: 89.2 us -> 78.8 us
  local copies, waits for them, and re-layouts: 0 us -> 1.46 us
    pallas_call x3 -> x1, Pallas kernels: 77 us -> 67.3 us  [shards(): pl.pallas_call(functools.partial(exchange_kernel, seq_count, capacity), o...]
    reshape x0 -> x1, local copies, waits for them, and re-layouts: none -> 1.46 us  [shards(): perm_blocks = cluster_perm.reshape(group_heads * shard_blocks, 1, BLOCK)]
where the time goes in v2:
time: 81.3 us; the launch traced here: 80.9 us
  Pallas kernels  78.8 us (97%)
  local copies, waits for them, and re-layouts  1.46 us (2%)
    pallas_call x1, Pallas kernels, shards(): pl.pallas_call(functools.partial(exchange_kernel, seq_count, capacity), o...  67.3 us
    pallas_call x1, Pallas kernels, shards(): pl.pallas_call(functools.partial(attend_kernel, group_heads, picks, slots...  9.58 us
    pallas_call x1, Pallas kernels, shards(): pl.pallas_call(functools.partial(routing_kernel, shard_blocks, capacity,...  1.9 us

profile of v2, /device:TPU:0, one launch (start us, length us, event | category | flops | bytes accessed | tf_op | source)
XLA Modules:
  0.0 80.9 jit_solution(4525714554697619276)
XLA Ops:
  0.0 0.7 pad_add_fusion.ids
  0.7 1.9 %routing.1 = (s32[16,1,128]{2,1,0:T(1,128)}, s32[20,128]{1,0:T(8,128)}) custom-call(s32[20,4,64]{2,1,0:T(4,128)} %mask_ref.1), custom_call_target="tpu_custom_call" | custom-call | tf_op jit(solution)/shard_map/routing/pallas_call | solution.py:318
  2.6 1.5 %reshape.6.perm_ref = s32[80,1,128]{2,1,0:T(1,128)} reshape(s32[20,512]{1,0:T(8,128)} %param.8) | data formatting | bytes 81920 | tf_op jit(solution)/shard_map/reshape | solution.py:325
  4.0 67.3 %exchange.1 = (bf16[2,16,2,128,256]{4,3,2,1,0:T(8,128)(2,1)}, s32[20,128]{1,0:T(8,128)}) custom-call(bf16[256,5120]{1,0:T(8,128)(2,1)} %key_ref.1, bf16[256,5120]{1,0:T(8,128)(2,1)} %value_ref.1, s32[80,1,128]{2,1,0:T(1,128)} %reshape.6.perm_ref, s32[16,1,128]{2,1,0:T(1,128)} %get-tuple-element.10.req_ref, s32[20,128]{1,0:T(8,128)} %get-tuple-element.9.pos_ref.pos_own), custom_call_target="tpu_custom_call" | custom-call | tf_op jit(solution)/shard_map/exchange/pallas_call | solution.py:327
  71.3 9.6 %attend.1 = bf16[256,5120]{1,0:T(8,128)(2,1)} custom-call(s32[2]{0:T(128)} %pad_add_fusion.ids, s32[20,128]{1,0:T(8,128)} %get-tuple-element.9.pos_ref.pos_own, s32[20,128]{1,0:T(8,128)} %get-tuple-element.11.pos_far, bf16[256,5120]{1,0:T(8,128)(2,1)} %refs_0_.1, bf16[64,128,256]{2,1,0:T(8,128)(2,1)} %bitcast.3), custom_call_target="tpu_custom_call" | custom-call | tf_op jit(solution)/shard_map/attend/pallas_call | solution.py:360

commit v3 on v2

--- a/solution.py
+++ b/solution.py
@@ -29,7 +29,7 @@
     return peer
 
 
-def routing_kernel(shard_blocks, capacity, picks, mask_ref, req_ref, pos_ref):
+def route(shard_blocks, capacity, picks, mask_ref, req_ref, pos_ref):
     heads, _, blocks = mask_ref.shape
     seq_count = blocks // shard_blocks
     needed = jnp.max(mask_ref[...], axis=1).astype(jnp.float32)
@@ -43,7 +43,7 @@
     lower = ones(iota((heads, heads), 1) < iota((heads, heads), 0))
     rank = dot(lower, by_owner) + before_in_owner
     head_ids, block_ids = iota((heads, blocks), 0), iota((heads, blocks), 1)
-    pair = (head_ids * shard_blocks + block_ids % shard_blocks).astype(jnp.float32)
+    pair = (block_ids % shard_blocks * heads + head_ids).astype(jnp.float32)
     slot_row = iota((128, blocks), 0)
     sums = jnp.zeros((128, blocks), jnp.float32)
     for c in range(capacity):
@@ -73,15 +73,16 @@
 
 
 def exchange_kernel(
-    seq_count, capacity,
-    key_ref, value_ref, perm_ref, req_ref, pos_ref, got_ref, pos_out,
-    near_kv, far_kv, asked_ref, asked, send_ref, rows_ref,
+    seq_count, capacity, shard_blocks, picks,
+    key_ref, value_ref, perm_ref, mask_ref, got_ref, pos_ref, pos_out,
+    near_key, near_value, far_key, far_value, req_ref, asked_ref, asked, send_ref, rows_ref, blocks_ref,
     load_sem, swap_send, swap_recv, req_send, req_recv, misc_sem,
     sends, recvs, relay_send, relay_recv,
 ):
     group, me = lax.axis_index("head"), lax.axis_index("seq")
     other = 1 - group
-    heads, rows = near_kv.shape[1:3]
+    near_kv, far_kv = (near_key, near_value), (far_key, far_value)
+    heads, rows = near_key.shape[:2]
     barrier = pltpu.get_barrier_semaphore()
     pl.semaphore_signal(barrier, inc=1, device_id={"head": other}, device_id_type=MESH)
 
@@ -98,7 +99,7 @@
             start_at = pl.multiple_of((group * heads + head) * HEAD_DIM, HEAD_DIM)
             loads.append(
                 pltpu.make_async_copy(
-                    src.at[:, pl.ds(start_at, HEAD_DIM)], near_kv.at[number, head],
+                    src.at[:, pl.ds(start_at, HEAD_DIM)], near_kv[number].at[head],
                     load_sem.at[number * heads + head],
                 )
             )
@@ -106,19 +107,6 @@
         copy.start()
     pl.semaphore_wait(barrier, seq_count)
 
-    def ask(step, landing):
-        peer = partner_of(me, step, seq_count)
-        return pltpu.make_async_remote_copy(
-            src_ref=req_ref.at[peer], dst_ref=asked_ref.at[peer if landing else me],
-            send_sem=req_send.at[step], recv_sem=req_recv.at[step],
-            device_id={"seq": peer}, device_id_type=MESH,
-        )
-
-    def start_ask(step, carry):
-        ask(step, False).start()
-        return carry
-
-    lax.fori_loop(1, seq_count, start_ask, 0)
     swaps = []
     for number, src in enumerate((key_ref, value_ref)):
         for head in range(heads):
@@ -126,13 +114,31 @@
             at = number * heads + head
             swaps.append(
                 pltpu.make_async_remote_copy(
-                    src_ref=src.at[:, pl.ds(start_at, HEAD_DIM)], dst_ref=far_kv.at[number, head],
+                    src_ref=src.at[:, pl.ds(start_at, HEAD_DIM)], dst_ref=far_kv[number].at[head],
                     send_sem=swap_send.at[at], recv_sem=swap_recv.at[at],
                     device_id={"head": other}, device_id_type=MESH,
                 )
             )
     for copy in swaps:
         copy.start()
+    route(shard_blocks, capacity, picks, mask_ref, req_ref, pos_ref)
+    for b in range(shard_blocks):
+        blocks_ref[b * heads : (b + 1) * heads] = perm_ref[:, b * BLOCK : (b + 1) * BLOCK][:, None, :]
+    rows_ref[...] = jnp.zeros_like(rows_ref)
+
+    def ask(step, landing):
+        peer = partner_of(me, step, seq_count)
+        return pltpu.make_async_remote_copy(
+            src_ref=req_ref.at[peer], dst_ref=asked_ref.at[peer if landing else me],
+            send_sem=req_send.at[step], recv_sem=req_recv.at[step],
+            device_id={"seq": peer}, device_id_type=MESH,
+        )
+
+    def start_ask(step, carry):
+        ask(step, False).start()
+        return carry
+
+    lax.fori_loop(1, seq_count, start_ask, 0)
     tell = pltpu.make_async_remote_copy(
         src_ref=pos_ref, dst_ref=pos_out, send_sem=misc_sem.at[0], recv_sem=misc_sem.at[1],
         device_id={"head": other}, device_id_type=MESH,
@@ -150,95 +156,101 @@
     to_scalar = pltpu.make_async_copy(asked_ref, asked, misc_sem.at[3])
     to_scalar.start()
     to_scalar.wait()
-    for copy in loads:
-        copy.wait()
-    for copy in swaps:
-        copy.wait()
-
     base = me * (2 * rows)
     token = iota((BLOCK, rows), 1)
     near = token + (base + group * rows)
     far = token + (base + other * rows)
-    rows_ref[...] = jnp.zeros_like(rows_ref)
-
-    def gather(peer):
+
+    def gather(which, peer):
         chosen = []
         for c in range(capacity):
-            rows_ref[c : c + 1, :] = perm_ref[asked[peer, 0, 2 * c]]
-            chosen.append(asked[peer, 0, 2 * c + 1])
+            pair = jnp.clip(asked[peer, 0, 2 * c], 0, heads * shard_blocks - 1)
+            rows_ref[c : c + 1, :] = blocks_ref[pair]
+            chosen.append(jnp.clip(asked[peer, 0, 2 * c + 1], 0, heads - 1))
         turned = rows_ref[...].T
         for c, head in enumerate(chosen):
             column = turned[:, c : c + 1]
             near_table = (column == near).astype(jnp.float32).astype(jnp.bfloat16)
             far_table = (column == far).astype(jnp.float32).astype(jnp.bfloat16)
-            for which in range(2):
-                got = jnp.dot(near_table, near_kv[which, head], preferred_element_type=jnp.float32)
-                got += jnp.dot(far_table, far_kv[which, head], preferred_element_type=jnp.float32)
-                send_ref[peer, c, :, which * HEAD_DIM : (which + 1) * HEAD_DIM] = got.astype(
-                    jnp.bfloat16
-                )
-
-    def deliver(step, landing):
+            got = jnp.dot(near_table, near_kv[which][head], preferred_element_type=jnp.float32)
+            got += jnp.dot(far_table, far_kv[which][head], preferred_element_type=jnp.float32)
+            send_ref[which, peer, c] = got.astype(jnp.bfloat16)
+
+    def deliver(which, step, landing):
         peer = partner_of(me, step, seq_count)
         return pltpu.make_async_remote_copy(
-            src_ref=send_ref.at[peer], dst_ref=got_ref.at[0, peer if landing else me],
-            send_sem=sends.at[step], recv_sem=recvs.at[step],
+            src_ref=send_ref.at[which, peer],
+            dst_ref=got_ref.at[0, which, peer if landing else me],
+            send_sem=sends.at[which, step], recv_sem=recvs.at[which, step],
             device_id={"seq": peer}, device_id_type=MESH,
         )
 
-    def relay(step):
+    def relay(which, step):
         peer = partner_of(me, step, seq_count)
         return pltpu.make_async_remote_copy(
-            src_ref=got_ref.at[0, peer], dst_ref=got_ref.at[1, peer],
-            send_sem=relay_send.at[step], recv_sem=relay_recv.at[step],
+            src_ref=got_ref.at[0, which, peer], dst_ref=got_ref.at[1, which, peer],
+            send_sem=relay_send.at[which, step], recv_sem=relay_recv.at[which, step],
             device_id={"head": other}, device_id_type=MESH,
         )
 
-    gather(partner_of(me, order(0, me, seq_count), seq_count))
-
-    def produce(i, carry):
-        gather(partner_of(me, order(i, me, seq_count), seq_count))
-        deliver(order(i - 1, me, seq_count), False).start()
+    for which in range(2):
+        for copy in loads[which * heads : (which + 1) * heads]:
+            copy.wait()
+        for copy in swaps[which * heads : (which + 1) * heads]:
+            copy.wait()
+        gather(which, partner_of(me, order(0, me, seq_count), seq_count))
+
+        def produce(i, carry, which=which):
+            gather(which, partner_of(me, order(i, me, seq_count), seq_count))
+            deliver(which, order(i - 1, me, seq_count), False).start()
+            return carry
+
+        lax.fori_loop(1, seq_count - 1, produce, 0)
+        gather(which, me)
+        deliver(which, order(seq_count - 2, me, seq_count), False).start()
+
+    locals_ = []
+    for which in range(2):
+        mine = pltpu.make_async_copy(
+            send_ref.at[which, me], got_ref.at[0, which, me], misc_sem.at[4 + which]
+        )
+        share = pltpu.make_async_remote_copy(
+            src_ref=send_ref.at[which, me], dst_ref=got_ref.at[1, which, me],
+            send_sem=relay_send.at[which, 0], recv_sem=relay_recv.at[which, 0],
+            device_id={"head": other}, device_id_type=MESH,
+        )
+        mine.start()
+        share.start()
+        locals_.extend((mine, share))
+
+    for which in range(2):
+
+        def pass_on(i, carry, which=which):
+            step = order(i, me, seq_count)
+            deliver(which, step, True).wait_recv()
+            relay(which, step).start()
+            return carry
+
+        lax.fori_loop(0, seq_count - 1, pass_on, 0)
+
+    def finish(step, carry):
+        for which in range(2):
+            deliver(which, step, True).wait_send()
+            relay(which, step).wait()
         return carry
 
-    lax.fori_loop(1, seq_count - 1, produce, 0)
-    gather(me)
-    deliver(order(seq_count - 2, me, seq_count), False).start()
-
-    def pass_on(i, carry):
-        step = order(i, me, seq_count)
-        deliver(step, True).wait_recv()
-        relay(step).start()
-        return carry
-
-    pass_on(0, 0)
-    mine = pltpu.make_async_copy(send_ref.at[me], got_ref.at[0, me], misc_sem.at[4])
-    mine.start()
-    share = pltpu.make_async_remote_copy(
-        src_ref=send_ref.at[me], dst_ref=got_ref.at[1, me],
-        send_sem=relay_send.at[0], recv_sem=relay_recv.at[0],
-        device_id={"head": other}, device_id_type=MESH,
-    )
-    share.start()
-    lax.fori_loop(1, seq_count - 1, pass_on, 0)
-
-    def finish(step, carry):
-        deliver(step, True).wait_send()
-        relay(step).wait()
-        return carry
-
     lax.fori_loop(1, seq_count, finish, 0)
-    mine.wait()
-    share.wait()
+    for copy in locals_:
+        copy.wait()
     tell.wait()
 
 
-def attend_kernel(heads, picks, slots, masked, ids, pos_own, pos_far, *refs):
+def attend_kernel(heads, picks, slots, masked, pos_own, pos_far, *refs):
     if masked:
         query_ref, kv_ref, allow_ref, out_ref = refs
     else:
         query_ref, kv_ref, out_ref = refs
-    group = ids[0]
+    group = lax.axis_index("head")
     width = query_ref.shape[1] // HEAD_DIM
     scale = 1.0 / math.sqrt(HEAD_DIM)
     slot_of, scores = [], []
@@ -248,10 +260,10 @@
         local = head % heads
         query = query_ref[:, w * HEAD_DIM : (w + 1) * HEAD_DIM]
         for p in range(picks):
-            slot = jnp.where(away, pos_far[local, p] + slots, pos_own[local, p])
+            slot = jnp.where(away, pos_far[local, p] + 2 * slots, pos_own[local, p])
             slot_of.append(slot)
             score = lax.dot_general(
-                query, kv_ref[slot, :, :HEAD_DIM], (((1,), (1,)), ((), ())),
+                query, kv_ref[slot], (((1,), (1,)), ((), ())),
                 preferred_element_type=jnp.float32,
             ) * scale
             if masked:
@@ -269,7 +281,7 @@
     for w in range(width):
         parts = [
             jnp.dot(
-                weights[w * picks + p], kv_ref[slot_of[w * picks + p], :, HEAD_DIM:],
+                weights[w * picks + p], kv_ref[slot_of[w * picks + p] + slots],
                 preferred_element_type=jnp.float32,
             )
             for p in range(picks)
@@ -307,44 +319,35 @@
     )
     slots = seq_count * capacity
     rows, columns = queries.shape
-    group, me = lax.axis_index("head"), lax.axis_index("seq")
-    ids = jnp.stack([group, me]).astype(jnp.int32)
+    me = lax.axis_index("seq")
     vmem = pl.BlockSpec(memory_space=pltpu.VMEM)
-    smem = pl.BlockSpec(memory_space=pltpu.SMEM)
     anywhere = pl.BlockSpec(memory_space=pl.ANY)
     struct = jax.ShapeDtypeStruct
     bf16, i32 = jnp.bfloat16, jnp.int32
 
-    requests, positions = pl.pallas_call(
-        functools.partial(routing_kernel, shard_blocks, capacity, picks),
-        out_shape=(struct((seq_count, 1, 128), i32), struct((group_heads, 128), i32)),
-        in_specs=[vmem], out_specs=(vmem, vmem), name="routing",
-    )(block_mask)
-
     dma = pltpu.SemaphoreType.DMA
-    perm_blocks = cluster_perm.reshape(group_heads * shard_blocks, 1, BLOCK)
-    kv_half = pltpu.VMEM((2, group_heads, rows, HEAD_DIM), bf16)
-    got, pos_far = pl.pallas_call(
-        functools.partial(exchange_kernel, seq_count, capacity),
-        out_shape=(
-            struct((2, seq_count, capacity, BLOCK, 2 * HEAD_DIM), bf16),
-            struct((group_heads, 128), i32),
-        ),
-        in_specs=[anywhere, anywhere, vmem, vmem, vmem],
-        out_specs=(anywhere, vmem),
+    kv_half = pltpu.VMEM((group_heads, rows, HEAD_DIM), bf16)
+    table = struct((group_heads, 128), i32)
+    got, positions, pos_far = pl.pallas_call(
+        functools.partial(exchange_kernel, seq_count, capacity, shard_blocks, picks),
+        out_shape=(struct((2, 2, seq_count, capacity, BLOCK, HEAD_DIM), bf16), table, table),
+        in_specs=[anywhere, anywhere, vmem, vmem],
+        out_specs=(anywhere, vmem, vmem),
         scratch_shapes=[
-            kv_half, kv_half,
+            kv_half, kv_half, kv_half, kv_half,
+            pltpu.VMEM((seq_count, 1, 128), i32),
             pltpu.VMEM((seq_count, 1, 128), i32),
             pltpu.SMEM((seq_count, 1, 128), i32),
-            pltpu.VMEM((seq_count, capacity, BLOCK, 2 * HEAD_DIM), bf16),
+            pltpu.VMEM((2, seq_count, capacity, BLOCK, HEAD_DIM), bf16),
             pltpu.VMEM((8 * -(-capacity // 8), 128), i32),
+            pltpu.VMEM((shard_blocks * group_heads, 1, BLOCK), i32),
             dma((2 * group_heads,)), dma((2 * group_heads,)), dma((2 * group_heads,)),
-            dma((seq_count,)), dma((seq_count,)), dma((5,)),
-        ] + [dma((seq_count,)) for _ in range(4)],
+            dma((seq_count,)), dma((seq_count,)), dma((6,)),
+        ] + [dma((2, seq_count)) for _ in range(4)],
         compiler_params=pltpu.CompilerParams(collective_id=0, has_side_effects=True),
         name="exchange",
-    )(key_states, value_states, perm_blocks, requests, positions)
-    got = got.reshape(2 * slots, BLOCK, 2 * HEAD_DIM)
+    )(key_states, value_states, cluster_perm, block_mask)
+    got = got.reshape(4 * slots, BLOCK, HEAD_DIM)
 
     masked = picks > 1
     total_heads = columns // HEAD_DIM
@@ -361,14 +364,14 @@
         functools.partial(attend_kernel, group_heads, picks, slots, masked),
         out_shape=struct((rows, columns), bf16),
         grid_spec=pltpu.PrefetchScalarGridSpec(
-            num_scalar_prefetch=3,
+            num_scalar_prefetch=2,
             grid=(total_heads // width,),
             in_specs=in_specs,
             out_specs=pl.BlockSpec((rows, width * HEAD_DIM), lambda i, *_: (0, i)),
         ),
         compiler_params=pltpu.CompilerParams(vmem_limit_bytes=56 * 1024 * 1024),
         name="attend",
-    )(ids, positions, pos_far, *operands)
+    )(positions, pos_far, *operands)
 
 
 def solution(mesh):

time: 81.3 us -> 75.1 us (0.924)
  Pallas kernels: 78.8 us -> 74.8 us
  local copies, waits for them, and re-layouts: 1.46 us -> 0 us
    pallas_call x2 -> x1, Pallas kernels: 69.2 us -> 65.2 us  [shards(): pl.pallas_call(functools.partial(exchange_kernel, seq_count, capacity, sh...]
    reshape x1 -> x0, local copies, waits for them, and re-layouts: 1.46 us -> none  [shards(): perm_blocks = cluster_perm.reshape(group_heads * shard_blocks, 1, BLOCK)]
where the time goes in v3:
time: 75.1 us; the launch traced here: 74.8 us
  Pallas kernels  74.8 us (100%)
    pallas_call x1, Pallas kernels, shards(): pl.pallas_call(functools.partial(exchange_kernel, seq_count, capacity, sh...  65.2 us
    pallas_call x1, Pallas kernels, shards(): pl.pallas_call(functools.partial(attend_kernel, group_heads, picks, slots...  9.57 us

profile of v3, /device:TPU:0, one launch (start us, length us, event | category | flops | bytes accessed | tf_op | source)
XLA Modules:
  0.0 74.8 jit_solution(8620030908084984712)
XLA Ops:
  0.0 65.2 %exchange.1 = (bf16[2,2,16,2,128,128]{5,4,3,2,1,0:T(8,128)(2,1)}, s32[20,128]{1,0:T(8,128)}, s32[20,128]{1,0:T(8,128)}) custom-call(bf16[256,5120]{1,0:T(8,128)(2,1)} %key_ref.1, bf16[256,5120]{1,0:T(8,128)(2,1)} %value_ref.1, s32[20,512]{1,0:T(8,128)} %perm_ref.1, s32[20,4,64]{2,1,0:T(4,128)} %mask_ref.1), custom_call_target="tpu_custom_call" | custom-call | tf_op jit(solution)/shard_map/exchange/pallas_call | solution.py:331
  65.2 9.6 %attend.1 = bf16[256,5120]{1,0:T(8,128)(2,1)} custom-call(s32[20,128]{1,0:T(8,128)} %get-tuple-element.8.pos_own, s32[20,128]{1,0:T(8,128)} %get-tuple-element.9.pos_far, bf16[256,5120]{1,0:T(8,128)(2,1)} %refs_0_.1, bf16[128,128,128]{2,1,0:T(8,128)(2,1)} %bitcast.1), custom_call_target="tpu_custom_call" | custom-call | tf_op jit(solution)/shard_map/attend/pallas_call | solution.py:363

commit v4 on v3

--- a/solution.py
+++ b/solution.py
@@ -74,7 +74,7 @@
 
 def exchange_kernel(
     seq_count, capacity, shard_blocks, picks,
-    key_ref, value_ref, perm_ref, mask_ref, got_ref, pos_ref, pos_out,
+    key_ref, value_ref, query_ref, perm_ref, mask_ref, got_ref, pos_ref, pos_out, query_out,
     near_key, near_value, far_key, far_value, req_ref, asked_ref, asked, send_ref, rows_ref, blocks_ref,
     load_sem, swap_send, swap_recv, req_send, req_recv, misc_sem,
     sends, recvs, relay_send, relay_recv,
@@ -144,6 +144,8 @@
         device_id={"head": other}, device_id_type=MESH,
     )
     tell.start()
+    stay = pltpu.make_async_copy(query_ref, query_out, misc_sem.at[6])
+    stay.start()
     keep = pltpu.make_async_copy(req_ref.at[me], asked_ref.at[me], misc_sem.at[2])
     keep.start()
     keep.wait()
@@ -243,52 +245,78 @@
     for copy in locals_:
         copy.wait()
     tell.wait()
-
-
-def attend_kernel(heads, picks, slots, masked, pos_own, pos_far, *refs):
+    stay.wait()
+
+
+def attend_kernel(heads, picks, width, capacity, masked, pos_own, pos_far, *refs):
     if masked:
-        query_ref, kv_ref, allow_ref, out_ref = refs
+        query_ref, kv_ref, allow_ref, out_ref, stage, sems = refs
     else:
-        query_ref, kv_ref, out_ref = refs
+        query_ref, kv_ref, out_ref, stage, sems = refs
     group = lax.axis_index("head")
-    width = query_ref.shape[1] // HEAD_DIM
-    scale = 1.0 / math.sqrt(HEAD_DIM)
-    slot_of, scores = [], []
-    for w in range(width):
-        head = pl.program_id(0) * width + w
-        away = (head // heads) != group
-        local = head % heads
-        query = query_ref[:, w * HEAD_DIM : (w + 1) * HEAD_DIM]
-        for p in range(picks):
-            slot = jnp.where(away, pos_far[local, p] + 2 * slots, pos_own[local, p])
-            slot_of.append(slot)
-            score = lax.dot_general(
-                query, kv_ref[slot], (((1,), (1,)), ((), ())),
-                preferred_element_type=jnp.float32,
-            ) * scale
-            if masked:
-                score = jnp.where(allow_ref[w, :, p : p + 1] > 0, score, -jnp.inf)
-            scores.append(score)
-    weights = []
-    for w in range(width):
-        own = scores[w * picks : (w + 1) * picks]
-        top = functools.reduce(jnp.maximum, [jnp.max(s, axis=1, keepdims=True) for s in own])
-        exps = [jnp.exp(s - top) for s in own]
-        total = functools.reduce(jnp.add, [jnp.sum(e, axis=1, keepdims=True) for e in exps])
-        inverse = 1.0 / total
-        weights.extend([(e * inverse).astype(jnp.bfloat16) for e in exps])
-    mixed = []
-    for w in range(width):
-        parts = [
-            jnp.dot(
-                weights[w * picks + p], kv_ref[slot_of[w * picks + p] + slots],
-                preferred_element_type=jnp.float32,
-            )
-            for p in range(picks)
-        ]
-        mixed.append(functools.reduce(jnp.add, parts).astype(jnp.bfloat16))
-    for w in range(width):
-        out_ref[:, w * HEAD_DIM : (w + 1) * HEAD_DIM] = mixed[w]
+    scale = math.log2(math.e) / math.sqrt(HEAD_DIM)
+    ones = jnp.ones((BLOCK, HEAD_DIM), jnp.bfloat16)
+    span = width * HEAD_DIM
+    batches = query_ref.shape[1] // span
+
+    def put(batch, buffer):
+        return pltpu.make_async_copy(
+            stage.at[buffer],
+            out_ref.at[:, pl.ds(pl.multiple_of(batch * span, span), span)],
+            sems.at[buffer],
+        )
+
+    def one(batch, carry):
+        where_, scores = [], []
+        for w in range(width):
+            head = batch * width + w
+            away = (head // heads) != group
+            local = head % heads
+            query = query_ref[:, pl.ds(pl.multiple_of(head * HEAD_DIM, HEAD_DIM), HEAD_DIM)]
+            for p in range(picks):
+                slot = jnp.where(away, pos_far[local, p], pos_own[local, p])
+                spot = (slot // capacity, slot % capacity)
+                rel = away.astype(jnp.int32)
+                where_.append((rel, spot))
+                score = lax.dot_general(
+                    query, kv_ref[rel, 0, spot[0], spot[1]], (((1,), (1,)), ((), ())),
+                    preferred_element_type=jnp.float32,
+                )
+                if masked:
+                    score = jnp.where(allow_ref[head, :, p : p + 1] > 0, score, -jnp.inf)
+                scores.append(score)
+        weights = []
+        for w in range(width):
+            own = scores[w * picks : (w + 1) * picks]
+            top = jnp.max(functools.reduce(jnp.maximum, own), axis=1, keepdims=True)
+            weights.extend([jnp.exp2((s - top) * scale).astype(jnp.bfloat16) for s in own])
+        buffer = batch % 2
+
+        @pl.when(batch >= 2)
+        def _():
+            put(batch - 2, buffer).wait()
+
+        for w in range(width):
+            parts = []
+            for p in range(picks):
+                rel, spot = where_[w * picks + p]
+                parts.append(
+                    jnp.dot(
+                        weights[w * picks + p],
+                        jnp.concatenate([kv_ref[rel, 1, spot[0], spot[1]], ones], axis=1),
+                        preferred_element_type=jnp.float32,
+                    )
+                )
+            mixed = functools.reduce(jnp.add, parts)
+            stage[buffer, :, w * HEAD_DIM : (w + 1) * HEAD_DIM] = (
+                mixed[:, :HEAD_DIM] / mixed[:, HEAD_DIM:]
+            ).astype(jnp.bfloat16)
+        put(batch, buffer).start()
+        return carry
+
+    lax.fori_loop(0, batches, one, 0)
+    for batch in range(max(0, batches - 2), batches):
+        put(batch, batch % 2).wait()
 
 
 def token_allow(cluster_perm, block_mask, picks, me, shard_rows):
@@ -317,22 +345,26 @@
     capacity = max(
         1, min(shard_blocks, (group_heads * picks * 8 + 5 * seq_count - 1) // (5 * seq_count))
     )
-    slots = seq_count * capacity
     rows, columns = queries.shape
     me = lax.axis_index("seq")
     vmem = pl.BlockSpec(memory_space=pltpu.VMEM)
-    anywhere = pl.BlockSpec(memory_space=pl.ANY)
+    anywhere = pl.BlockSpec(memory_space=pltpu.HBM)
     struct = jax.ShapeDtypeStruct
     bf16, i32 = jnp.bfloat16, jnp.int32
 
     dma = pltpu.SemaphoreType.DMA
     kv_half = pltpu.VMEM((group_heads, rows, HEAD_DIM), bf16)
     table = struct((group_heads, 128), i32)
-    got, positions, pos_far = pl.pallas_call(
+    resident = 2 * (4 * seq_count * capacity * BLOCK * HEAD_DIM + rows * columns)
+    grant = 67043328 - resident - 256 * 1024
+    got, positions, pos_far, near_queries = pl.pallas_call(
         functools.partial(exchange_kernel, seq_count, capacity, shard_blocks, picks),
-        out_shape=(struct((2, 2, seq_count, capacity, BLOCK, HEAD_DIM), bf16), table, table),
-        in_specs=[anywhere, anywhere, vmem, vmem],
-        out_specs=(anywhere, vmem, vmem),
+        out_shape=(
+            pltpu.VMEM((2, 2, seq_count, capacity, BLOCK, HEAD_DIM), bf16), table, table,
+            pltpu.VMEM((rows, columns), bf16),
+        ),
+        in_specs=[anywhere, anywhere, anywhere, vmem, vmem],
+        out_specs=(vmem, vmem, vmem, vmem),
         scratch_shapes=[
             kv_half, kv_half, kv_half, kv_half,
             pltpu.VMEM((seq_count, 1, 128), i32),
@@ -342,34 +374,28 @@
             pltpu.VMEM((8 * -(-capacity // 8), 128), i32),
             pltpu.VMEM((shard_blocks * group_heads, 1, BLOCK), i32),
             dma((2 * group_heads,)), dma((2 * group_heads,)), dma((2 * group_heads,)),
-            dma((seq_count,)), dma((seq_count,)), dma((6,)),
+            dma((seq_count,)), dma((seq_count,)), dma((7,)),
         ] + [dma((2, seq_count)) for _ in range(4)],
-        compiler_params=pltpu.CompilerParams(collective_id=0, has_side_effects=True),
+        compiler_params=pltpu.CompilerParams(
+            collective_id=0, has_side_effects=True, vmem_limit_bytes=grant
+        ),
         name="exchange",
-    )(key_states, value_states, cluster_perm, block_mask)
-    got = got.reshape(4 * slots, BLOCK, HEAD_DIM)
+    )(key_states, value_states, queries, cluster_perm, block_mask)
 
     masked = picks > 1
     total_heads = columns // HEAD_DIM
     width = 8 if total_heads % 8 == 0 else 1
-    in_specs = [
-        pl.BlockSpec((rows, width * HEAD_DIM), lambda i, *_: (0, i)),
-        pl.BlockSpec(got.shape, lambda i, *_: (0, 0, 0)),
-    ]
-    operands = [queries, got]
+    operands = [near_queries, got]
     if masked:
-        in_specs.append(pl.BlockSpec((width, rows, picks), lambda i, *_: (i, 0, 0)))
         operands.append(token_allow(cluster_perm, block_mask, picks, me, shard_rows))
+    smem = pl.BlockSpec(memory_space=pltpu.SMEM)
     return pl.pallas_call(
-        functools.partial(attend_kernel, group_heads, picks, slots, masked),
+        functools.partial(attend_kernel, group_heads, picks, width, capacity, masked),
         out_shape=struct((rows, columns), bf16),
-        grid_spec=pltpu.PrefetchScalarGridSpec(
-            num_scalar_prefetch=2,
-            grid=(total_heads // width,),
-            in_specs=in_specs,
-            out_specs=pl.BlockSpec((rows, width * HEAD_DIM), lambda i, *_: (0, i)),
-        ),
-        compiler_params=pltpu.CompilerParams(vmem_limit_bytes=56 * 1024 * 1024),
+        in_specs=[smem, smem] + [vmem] * len(operands),
+        out_specs=anywhere,
+        scratch_shapes=[pltpu.VMEM((2, rows, width * HEAD_DIM), bf16), dma((2,))],
+        compiler_params=pltpu.CompilerParams(vmem_limit_bytes=24 * 1024 * 1024),
         name="attend",
     )(positions, pos_far, *operands)
 

time: 75.1 us -> 73.1 us (0.973)
  Pallas kernels: 74.8 us -> 71.4 us
  local copies, waits for them, and re-layouts: 0 us -> 1.41 us
    pallas_call x1, Pallas kernels: 9.57 us -> 6.65 us  [shards(): pl.pallas_call(functools.partial(attend_kernel, group_heads, picks, width...]
    unnamed x0 -> x4, local copies, waits for them, and re-layouts: none -> 1.41 us
where the time goes in v4:
time: 73.1 us; the launch traced here: 72.8 us
  Pallas kernels  71.4 us (98%)
  local copies, waits for them, and re-layouts  1.41 us (2%)
    pallas_call x1, Pallas kernels, shards(): pl.pallas_call(functools.partial(exchange_kernel, seq_count, capacity, sh...  64.7 us
    pallas_call x1, Pallas kernels, shards(): pl.pallas_call(functools.partial(attend_kernel, group_heads, picks, width...  6.65 us

profile of v4, /device:TPU:0, one launch (start us, length us, event | category | flops | bytes accessed | tf_op | source)
XLA Modules:
  0.0 72.8 jit_solution(1667260382164172901)
XLA Ops:
  0.0 64.7 %exchange.1 = (bf16[2,2,16,2,128,128]{5,4,3,2,1,0:T(8,128)(2,1)S(1)}, s32[20,128]{1,0:T(8,128)}, s32[20,128]{1,0:T(8,128)}, bf16[256,5120]{1,0:T(8,128)(2,1)S(1)}) custom-call(bf16[256,5120]{1,0:T(8,128)(2,1)} %key_ref.1, bf16[256,5120]{1,0:T(8,128)(2,1)} %value_ref.1, bf16[256,5120]{1,0:T(8,128)(2,1)} %query_ref.1, s32[20,512]{1,0:T(8,128)} %perm_ref.1, ...), custom_call_target="tpu_custom_call" | custom-call | tf_op jit(solution)/shard_map/exchange/pallas_call | solution.py:360
  64.7 0.0 copy-start
  64.7 0.7 copy-done
  65.4 0.0 copy-start.1
  65.4 0.7 copy-done.1
  66.1 6.7 %attend.1 = bf16[256,5120]{1,0:T(8,128)(2,1)} custom-call(s32[20,128]{1,0:T(8,128)S(1)} %copy-done, s32[20,128]{1,0:T(8,128)S(1)} %copy-done.1, bf16[256,5120]{1,0:T(8,128)(2,1)S(1)} %get-tuple-element.11.refs_0_, bf16[2,2,16,2,128,128]{5,4,3,2,1,0:T(8,128)(2,1)S(1)} %get-tuple-element.12.refs_1_), custom_call_target="tpu_custom_call" | custom-call | tf_op jit(solution)/shard_map/attend/pallas_call | solution.py:392
Async XLA Ops:
  64.7 0.7 copy-start
  65.4 0.7 copy-start.1
